TPU v7x, 128 devices: a whole 4x4x4 slice. The times are simulated.
128 devices in a mesh: video: 32 (over z_hi, x, y), head: 4 (over z_lo, core).
Axes of the slice: x: 4, y: 4, z: 4 (z_hi: 2, z_lo: 2; z = z_hi * 2 + z_lo), core: 2. Of those that a mesh axis runs over, the one named last changes fastest.
Arguments:
- text_queries: bfloat16 [512, 8192], P('video', 'head'), may hold values from -140 to 140
- visual_keys: bfloat16 [16384, 1024], P('video', 'head'), may hold values from -5 to 5
- visual_values: bfloat16 [16384, 1024], P('video', 'head'), may hold values from -6 to 6
- out_grad: bfloat16 [512, 8192], P('video', 'head'), may hold values from -1536 to 1536
- query_frame: int32 [512], replicated, may hold values from 0 to 15
- block_frame: int32 [128], replicated, may hold values from 0 to 16, as said below
- q_weight: bfloat16 [8192, 8192], P('head', 'video'), may hold values from -0.0625 to 0.0625
Outputs:
- query_grad: bfloat16 [512, 8192], P('video', 'head')
- key_grad: bfloat16 [16384, 1024], P('video', 'head')
- value_grad: bfloat16 [16384, 1024], P('video', 'head')
- text_grad: bfloat16 [512, 8192], P('head', 'video')
Inputs may be any that keep to these rules, and one draw needn't show every extreme that they name: `block_frame`: on each index of video the first 1 to 4 block slots are live and the rest empty; some index has all 4 live. Live blocks carry frame numbers that never fall along the whole array and start at 0; empty slots carry 16.
All inputs are finite; a program needn't handle non-finite values.
Results may differ from a plain program's by a relative error of at most 0.0058.
Values may be sent and summed in bfloat16 or wider, within the bound.
No kernel may reach another device: no remote copies, remote signals or barrier semaphores. Data moves between devices by JAX's collectives and lax.ppermute only.
A program may use at most 384 MiB of HBM per device.

v0:
```python
import jax
import jax.numpy as jnp
from jax import lax
from jax.sharding import Mesh
from jax.sharding import PartitionSpec as P

HEADS = 64
KV_HEADS = 8
HEAD_DIM = 128
BLOCK = 128
VIDEO = ("video_0", "video_1", "video_2")


neg_fill = -1e30


def side_by_side(arrays, axis, dim, along):
    both = jnp.concatenate(arrays, axis=along)
    filled, at, outs = (lax.all_gather(both, axis, axis=dim, tiled=True), 0, [])
    for a in arrays:
        outs.append(lax.slice_in_dim(filled, at, at + a.shape[along], axis=along))
        at += a.shape[along]
    return tuple(outs)


def joined_all(x, axes, combine):
    for axis in axes:
        pieces = jax.tree.map(lambda part: lax.all_gather(part, axis), x)
        x = jax.tree.map(lambda part: part[0], pieces)
        for k in range(1, lax.axis_size(axis)):
            x = combine(x, jax.tree.map(lambda part: part[k], pieces))
    return x


def split_queries(source):
    return source.reshape(source.shape[0], -1, HEADS // KV_HEADS, HEAD_DIM)


def row_frames(block_frame, row_start, piece_rows):
    row_index = row_start + jnp.arange(piece_rows, dtype=jnp.int32)
    return jnp.take(block_frame, row_index // BLOCK)


def key_layout(key_piece, value_piece, frame_rows):
    piece_rows = key_piece.shape[0]
    block_rows = BLOCK
    block_count = piece_rows // block_rows
    local_heads = key_piece.shape[1] // HEAD_DIM
    shaped_keys = key_piece.reshape(block_count, block_rows, local_heads, HEAD_DIM)
    shaped_values = value_piece.reshape(block_count, block_rows, local_heads, HEAD_DIM)
    return (shaped_keys, shaped_values, frame_rows.reshape(block_count, block_rows))


def masked_scores(query_heads, query_limit, key_block, frame_block):
    scores = jnp.einsum(
        "rgjd,kgd->rgjk", query_heads, key_block, preferred_element_type=jnp.float32
    ) * HEAD_DIM ** (-0.5)
    visible = (frame_block[None, :] <= query_limit[:, None])[:, None, None, :]
    return (jnp.where(visible, scores, neg_fill), visible)


def sweep(block_step, running, layout, grads_in):
    shaped_keys, shaped_values, shaped_frames = layout

    def visit_block(state_now, block_items):
        key_block, value_block, frame_block, grads_block = block_items
        return block_step(state_now, key_block, value_block, frame_block, grads_block)

    return lax.scan(visit_block, running, (shaped_keys, shaped_values, shaped_frames, grads_in))


def forward_step(query_heads, query_limit):

    def block_step(running, key_block, value_block, frame_block, grads_in):
        peaks, totals, weighted = running
        scores, visible = masked_scores(query_heads, query_limit, key_block, frame_block)
        new_peak = jnp.maximum(peaks, jnp.max(scores, axis=-1))
        rescale = jnp.exp(peaks - new_peak)
        weights = jnp.where(visible, jnp.exp(scores - new_peak[..., None]), 0.0)
        totals = totals * rescale + jnp.sum(weights, axis=-1)
        weighted = weighted * rescale[..., None] + jnp.einsum(
            "rgjk,kgd->rgjd",
            weights,
            value_block.astype(jnp.float32),
            precision=lax.Precision.HIGHEST,
        )
        return ((new_peak, totals, weighted), grads_in)

    return block_step


def backward_step(query_heads, grad_heads, query_limit, log_total, row_dots):

    def block_step(running, key_block, value_block, frame_block, grads_in):
        scores, visible = masked_scores(query_heads, query_limit, key_block, frame_block)
        weights = jnp.where(visible, jnp.exp(scores - log_total[..., None]), 0.0)
        value_dots = jnp.einsum(
            "rgjd,kgd->rgjk", grad_heads, value_block, preferred_element_type=jnp.float32
        )
        score_grads = (weights * (value_dots - row_dots[..., None])).astype(jnp.bfloat16)
        running = running + jnp.einsum(
            "rgjk,kgd->rgjd", score_grads, key_block, preferred_element_type=jnp.float32
        ) * HEAD_DIM ** (-0.5)
        weight_half = weights.astype(jnp.bfloat16)
        key_part = jnp.einsum(
            "rgjk,rgjd->kgd", score_grads, query_heads, preferred_element_type=jnp.float32
        ) * HEAD_DIM ** (-0.5)
        value_part = jnp.einsum(
            "rgjk,rgjd->kgd", weight_half, grad_heads, preferred_element_type=jnp.float32
        )
        grads_in = (grads_in[0] + key_part, grads_in[1] + value_part)
        return (running, grads_in)

    return block_step


def initial_state(total_rows, local_heads):
    group_size = HEADS // KV_HEADS
    return (
        jnp.full((total_rows, local_heads, group_size), neg_fill, jnp.float32),
        jnp.zeros((total_rows, local_heads, group_size), jnp.float32),
        jnp.zeros((total_rows, local_heads, group_size, HEAD_DIM), jnp.float32),
    )


def combine_parts(earlier, later):
    new_peak = jnp.maximum(earlier[0], later[0])
    early_scale = jnp.exp(earlier[0] - new_peak)
    late_scale = jnp.exp(later[0] - new_peak)
    totals = earlier[1] * early_scale + later[1] * late_scale
    weighted = earlier[2] * early_scale[..., None] + later[2] * late_scale[..., None]
    return (new_peak, totals, weighted)


def shards(text_queries, visual_keys, visual_values, out_grad, query_frame, block_frame, q_weight):
    query_rows = text_queries.shape[0]
    key_rows = visual_keys.shape[0]
    local_heads = visual_keys.shape[1] // HEAD_DIM
    video_index = lax.axis_index(VIDEO)
    own_frames = row_frames(block_frame, video_index * key_rows, key_rows)
    own_layout = key_layout(visual_keys, visual_values, own_frames)
    grad_shape = own_layout[0].shape[:2] + (local_heads, HEAD_DIM)
    all_queries, all_grads = side_by_side((text_queries, out_grad), VIDEO, 0, 1)
    total_rows = all_queries.shape[0]
    query_heads = split_queries(all_queries)
    grad_heads = split_queries(all_grads)
    partial_value, unused = sweep(
        forward_step(query_heads, query_frame),
        initial_state(total_rows, local_heads),
        own_layout,
        (),
    )
    peaks, totals, weighted = joined_all(partial_value, VIDEO, combine_parts)
    row_dots = jnp.sum(grad_heads * (weighted / totals[..., None]), axis=-1)
    log_total = peaks + jnp.log(totals)
    zero_grads = (jnp.zeros(grad_shape, jnp.float32), jnp.zeros(grad_shape, jnp.float32))
    query_start = jnp.zeros(partial_value[2].shape, jnp.float32)
    block_step = backward_step(query_heads, grad_heads, query_frame, log_total, row_dots)
    query_sum, key_value = sweep(block_step, query_start, own_layout, zero_grads)
    query_total = lax.psum(query_sum, VIDEO)
    query_grad_all = query_total.reshape(total_rows, -1).astype(jnp.bfloat16)
    query_grad = lax.dynamic_slice_in_dim(query_grad_all, video_index * query_rows, query_rows, 0)
    key_sum, value_sum = key_value
    key_grad = key_sum.reshape(key_rows, -1).astype(jnp.bfloat16)
    value_grad = value_sum.reshape(key_rows, -1).astype(jnp.bfloat16)
    partial_text = jnp.dot(query_grad_all, q_weight, preferred_element_type=jnp.float32)
    text_grad = lax.psum_scatter(partial_text, "head", scatter_dimension=0, tiled=True).astype(
        jnp.bfloat16
    )
    return (query_grad, key_grad, value_grad, text_grad)


def solution(mesh):
    split = Mesh(
        mesh.devices.reshape(2, 4, 4, mesh.shape["head"]), ("video_0", "video_1", "video_2", "head")
    )
    placed = (
        P(VIDEO, "head"),
        P(VIDEO, "head"),
        P(VIDEO, "head"),
        P(VIDEO, "head"),
        P(),
        P(),
        P("head", VIDEO),
    )
    return jax.shard_map(
        shards,
        mesh=split,
        in_specs=placed,
        out_specs=(P(VIDEO, "head"), P(VIDEO, "head"), P(VIDEO, "head"), P("head", VIDEO)),
        check_vma=False,
    )
```

profile of v0, /device:TPU:1, one launch (start us, length us, event | category | flops | bytes accessed | tf_op | source)
XLA Modules:
  0.0 959.7 jit_solution(10768328933219193713)
XLA Ops:
  7.2 1.6 pad_maximum_fusion
  10.7 1.7 reshape.389
  12.5 3.4 gather_fusion
  15.9 79.9 %all-gather.8.cloned.1.call-done = bf16[512,4096]{1,0:T(8,128)(2,1)} async-done(((bf16[16,4096]{1,0:T(8,128)(2,1)}), bf16[512,4096]{1,0:T(8,128)(2,1)}) %all-gather.8.cloned.1.call-update) | async-done | bytes 4194320 | tf_op jit(solution)/shard_map/all_gather | solution.py:19
  95.8 4.2 fusion.98
  100.0 2.5 copy.104
  102.5 3.0 copy.84
  105.6 67.9 %while.30 = (s32[]{:T(128)}, f32[512,2,8]{0,2,1:T(8,128)S(1)}, f32[512,2,8]{0,2,1:T(8,128)S(1)}, f32[512,2,8,128]{0,3,2,1:T(8,128)}, s32[4,128]{1,0:T(4,128)S(1)...) while((s32[]{:T(128)}, f32[512,2,8]{0,2,1:T(8,128)S(1)}, ...), condition=%wide.region_3.4_spmd.clone, body=%wide.region_0.0_spmd.clone.sunk | while | flops 1894883328 | bytes 24252544 | solution.py:69
  105.7 3.7 fusion.132
  109.4 3.2 fusion.133
  113.7 7.9 bitcast_add_fusion.4
  121.7 3.7 fusion.132
  125.4 3.2 fusion.133
  129.7 9.2 bitcast_add_fusion.4
  139.0 3.7 fusion.132
  142.7 3.2 fusion.133
  147.0 9.2 bitcast_add_fusion.4
  156.3 3.7 fusion.132
  160.0 3.2 fusion.133
  164.3 9.2 bitcast_add_fusion.4
  173.5 5.5 copy.70
  179.0 4.9 all-gather
  186.0 99.7 %all-gather.14.cloned.1.call-done = f32[1024,2,8,128]{3,2,1,0:T(8,128)} async-done(((f32[512,2,8,128]{3,2,1,0:T(8,128)}), f32[1024,2,8,128]{3,2,1,0:T(8,128)}) %all-gather.14.cloned.1.call-update) | async-done | bytes 8388624 | tf_op jit(solution)/shard_map/all_gather | solution.py:28
  285.7 8.0 fusion.53
  293.8 4.9 all-gather.1
  299.4 9.4 all_gather.48
  314.9 132.3 %all-gather.10.cloned.1.call-done = f32[4,512,2,8,128]{4,3,2,1,0:T(8,128)} async-done(((f32[1,512,2,8,128]{4,3,2,1,0:T(8,128)}), f32[4,512,2,8,128]{4,3,2,1,0:T(8,128)}) %all-gather.10.cloned.1.call-update) | async-done | bytes 16777232 | tf_op jit(solution)/shard_map/all_gather | solution.py:28
  447.2 11.6 %fusion.47 = f32[1,512,2,8,128]{4,3,2,1,0:T(8,128)} fusion(f32[4,512,2,8,128]{4,3,2,1,0:T(8,128)} %all-gather.10.cloned.1.call-done, f32[512,2,8]{2,1,0:T(2,128)} %copy.78, f32[512,2,8]{2,1,0:T(2,128)} %copy.77, f32[512,2,8]{2,1,0:T(2,128)} %copy.76, f32[512,2,8]{2,1,0:T(2,128)} %copy.75, f32[512,2,8]{2,1,0:T(2,128)} %copy.74, f32[512,2,8]{2,1,0:T(2,128)} %copy.73), kind=kLoop, calls=%fused_computation.62 | loop fusion | flops 9437184 | bytes 21168128 | tf_op jit(solution)/shard_map/add | solution.py:131
  458.9 4.0 copy.105
  462.8 4.0 copy.86
  466.8 9.4 all_gather.52
  476.2 11.5 %all_gather.49 = f32[4,512,2,8]{1,3,2,0:T(8,128)S(1)} all-gather(f32[1,512,2,8]{1,3,2,0:T(8,128)S(1)} %get-tuple-element.319), channel_id=1, replica_groups=mesh['video_0'=2,'video_1'=4,'video_2'=4,'head'=4] {'video_2'}, dimensions={0}, use_global_device_ids=true | all-gather | bytes 163840 | tf_op jit(solution)/shard_map/all_gather | solution.py:28
  487.6 11.0 %all_gather.53 = f32[4,512,2,8]{1,3,2,0:T(8,128)S(1)} all-gather(f32[1,512,2,8]{1,3,2,0:T(8,128)S(1)} %get-tuple-element.318), channel_id=1, replica_groups=mesh['video_0'=2,'video_1'=4,'video_2'=4,'head'=4] {'video_2'}, dimensions={0}, use_global_device_ids=true | all-gather | bytes 163840 | tf_op jit(solution)/shard_map/all_gather | solution.py:28
  499.4 116.7 %all-gather.12.cloned.1.call-done = f32[4,512,2,8,128]{4,3,2,1,0:T(8,128)} async-done(((f32[1,512,2,8,128]{4,3,2,1,0:T(8,128)}), f32[4,512,2,8,128]{4,3,2,1,0:T(8,128)}) %all-gather.12.cloned.1.call-update) | async-done | bytes 16777232 | tf_op jit(solution)/shard_map/all_gather | solution.py:28
  616.1 12.2 %fusion.97 = (f32[1,512,2,8,128]{4,3,2,1,0:T(8,128)}, f32[1,512,2,8,128]{4,3,2,1,0:T(8,128)}, f32[1,512,2,8,128]{4,3,2,1,0:T(8,128)}, f32[1,512,2,8,128]{4,3,2,1,0:T(8,128)}) fusion(f32[4,512,2,8,128]{4,3,2,1,0:T(8,128)} %all-gather.12.cloned.1.call-done), kind=kLoop, calls=%fused_computation.174 | loop fusion | bytes 33554432 | tf_op jit(solution)/shard_map/slice | solution.py:29
  628.3 5.3 copy.106
  633.6 5.3 copy.107
  638.9 5.3 copy.108
  644.2 5.3 copy.109
  649.5 8.5 fusion.62
  658.0 64.7 %while.31 = (s32[]{:T(128)}, f32[512,2,8,128]{0,3,2,1:T(8,128)}, bf16[4,128,2,128]{3,1,2,0:T(8,128)(2,1)S(1)}, bf16[4,128,2,128]{3,1,2,0:T(8,128)(2,1)}, bf16[4,...) while((s32[]{:T(128)}, f32[512,2,8,128]{0,3,2,1:T(8,128)}, ...), condition=%wide.region_6.7_spmd.clone, body=%wide.region_5.6_spmd.clone.sunk | while | flops 1358004224 | bytes 95524192 | solution.py:69
  658.0 1.7 fusion.144
  661.7 2.9 fusion.146
  664.6 4.5 bitcast_add_fusion.5
  671.3 1.9 fusion.148
  673.3 1.7 fusion.144
  676.9 2.9 fusion.146
  679.9 5.7 bitcast_add_fusion.5
  687.8 1.9 fusion.148
  689.7 1.7 fusion.144
  693.4 2.9 fusion.146
  696.3 5.7 bitcast_add_fusion.5
  704.3 1.9 fusion.148
  706.2 1.7 fusion.144
  709.9 2.9 fusion.146
  712.8 5.7 bitcast_add_fusion.5
  720.7 1.9 fusion.148
  722.7 188.4 %all-reduce.1 = bf16[512,2,8,128]{0,3,2,1:T(8,128)(2,1)S(1)} all-reduce(f32[512,2,8,128]{0,3,2,1:T(8,128)} %get-tuple-element.120), channel_id=1, replica_groups=mesh['video_0'=2,'video_1'=4,'video_2'=4,'head'=4] {'video_0','video_1',..., use_global_device_ids=true, to_apply=%region_7.8 | all-reduce | flops 1048576 | bytes 6291456 | tf_op jit(solution)/shard_map/psum | solution.py:160
  911.1 1.6 fusion.99
  913.9 1.9 copy.89
  916.9 1.8 copy.110
  918.7 1.8 copy_bitcast_fusion.2
  920.5 31.1 %reduce-scatter.2.cloned.1.call-done = f32[128,256]{1,0:T(8,128)} async-done(((f32[512,256]{1,0:T(8,128)}), f32[128,256]{1,0:T(8,128)}) %reduce-scatter.2.cloned.1.call-update) | async-done | bytes 131088 | tf_op jit(solution)/shard_map/reduce_scatter | solution.py:167
  951.7 1.5 convert_element_type.38
  (144 shorter events, 35.0 us)
Async XLA Ops:
  7.2 904.0 %copy-start = (bf16[2048,256]{1,0:T(8,128)(2,1)S(1)}, bf16[2048,256]{1,0:T(8,128)(2,1)}, u32[]{:S(2)}) copy-start(bf16[2048,256]{1,0:T(8,128)(2,1)} %param.17) | copy-start | bytes 3145732
  7.2 88.7 %all-gather.8.cloned.1.call-start = ((), (), s32[]{:S(2)}) async-start(), calls=%async_computation.1 | async-start | bytes 4325376 | tf_op jit(solution)/shard_map/all_gather | solution.py:19
  8.9 276.9 %all-gather.14.cloned.1.call-start = ((), (), s32[]{:S(2)}) async-start(), calls=%async_computation.5 | async-start | bytes 12582912 | tf_op jit(solution)/shard_map/all_gather | solution.py:28
  100.0 5.6 copy-start.7
  179.0 268.2 %all-gather.10.cloned.1.call-start = ((), (), s32[]{:S(2)}) async-start(), calls=%async_computation.2 | async-start | bytes 20971520 | tf_op jit(solution)/shard_map/all_gather | solution.py:28
  293.7 322.4 %all-gather.12.cloned.1.call-start = ((), (), s32[]{:S(2)}) async-start(), calls=%async_computation.3 | async-start | bytes 20971520 | tf_op jit(solution)/shard_map/all_gather | solution.py:28
  458.8 492.9 %reduce-scatter.2.cloned.1.call-start = ((), (), s32[]{:S(2)}) async-start(), calls=%async_computation.4 | async-start | bytes 655360 | tf_op jit(solution)/shard_map/reduce_scatter | solution.py:167
  658.0 3.7 copy-start.4
  658.0 3.7 copy-start.8
  658.0 3.7 copy-start.9
  659.7 1.9 copy-start.2
  664.6 4.5 copy-start.1
  664.6 5.2 copy-start.5
  669.1 2.2 copy-start.3
  673.3 3.7 copy-start.4
  673.3 3.7 copy-start.8
  673.3 3.7 copy-start.9
  675.0 1.9 copy-start.2
  679.9 5.8 copy-start.1
  679.9 6.5 copy-start.5
  685.6 2.2 copy-start.3
  689.7 3.7 copy-start.4
  689.7 3.7 copy-start.8
  689.7 3.7 copy-start.9
  691.4 1.9 copy-start.2
  696.3 5.8 copy-start.1
  696.3 6.5 copy-start.5
  702.1 2.2 copy-start.3
  706.2 3.7 copy-start.4
  706.2 3.7 copy-start.8
  706.2 3.7 copy-start.9
  707.9 1.9 copy-start.2
  712.8 5.8 copy-start.1
  712.8 6.5 copy-start.5
  718.5 2.2 copy-start.3
  722.7 190.0 %copy-start.6 = (bf16[4,128,2,128]{3,1,2,0:T(8,128)(2,1)}, bf16[4,128,2,128]{3,1,2,0:T(8,128)(2,1)S(1)}, u32[]{:S(2)}) copy-start(bf16[4,128,2,128]{3,1,2,0:T(8,128)(2,1)S(1)} %get-tuple-element.121) | copy-start | bytes 786436
Sparse Core Ops, SparseCore 0:
  11.7 84.1 all-gather.7
  179.1 106.5 all-gather.13
  293.9 153.2 all-gather.9
  458.9 157.1 all-gather.11
  912.8 38.8 reduce-scatter.1
where the time goes:
time: 962 us; the launch traced here: 960 us
  waiting for transfers between devices  460 us (48%)
  blocking collectives  240 us (25%)
  matrix products  103 us (11%)
  local copies, waits for them, and re-layouts  96.6 us (10%)
  other arithmetic  46.6 us (5%)
  between operations  13.9 us (1%)
    all_gather x3, waiting for transfers between devices, joined_all(): pieces = jax.tree.map(lambda part: lax.all_gather(part, axis), x)  349 us
    psum x1, blocking collectives, shards(): query_total = lax.psum(query_sum, VIDEO)  188 us
    all_gather x1, waiting for transfers between devices, side_by_side(): filled, at, outs = (lax.all_gather(both, axis, axis=dim, tiled=True), 0, [])  79.9 us
    all_gather x6, blocking collectives, joined_all(): pieces = jax.tree.map(lambda part: lax.all_gather(part, axis), x)  51.1 us
    unnamed x16, local copies, waits for them, and re-layouts  37.2 us
    dot_general x4, matrix products, block_step(): jnp.einsum('rgjk,kgd->rgjd', weights, value_block.astype(jnp.float32), pr...  35.5 us
    reduce_scatter x1, waiting for transfers between devices, shards(): lax.psum_scatter(partial_text, 'head', scatter_dimension=0, tiled=True)  31.1 us
    dot_general x4, matrix products, block_step(): jnp.einsum('rgjk,kgd->rgjd', score_grads, key_block, preferred_element_ty...  21.8 us
  transfers between devices with their start and end apart: 5, of which 5 were waited for; matrix products, arithmetic and copies ran while one was open for 3% of the time, Pallas kernels for 0%

commit v1 on v0

v1 whole, which is shorter than its diff:
```python
import functools
import math

import jax
import jax.numpy as jnp
from jax import lax
from jax.experimental import pallas as pl
from jax.experimental.pallas import tpu as pltpu
from jax.sharding import Mesh
from jax.sharding import PartitionSpec as P

HEADS = 64
KV_HEADS = 8
GROUP = HEADS // KV_HEADS
HEAD_DIM = 128
BLOCK = 128
VIDEO = ("vz", "vx", "vy")
PLANE = ("vx", "vy")
SCALE = HEAD_DIM ** -0.5
SCALE2 = SCALE * math.log2(math.e)
NEG = -1.0e30
CONTRACT_LAST = (((1,), (1,)), ((), ()))


def dot_last(a, b):
    return lax.dot_general(a, b, CONTRACT_LAST, preferred_element_type=jnp.float32)


def dot(a, b):
    return jnp.dot(a, b, preferred_element_type=jnp.float32)


def fold(x):
    return x.reshape(x.shape[0] // 8, 8, x.shape[1])


def forward_kernel(frames, limit, q, do, k0, v0, k1, v1, stats, scores):
    head = pl.program_id(0)
    queries = q[...]
    grads = do[...]
    limits = limit[...]
    half = k0.shape[0] // BLOCK
    top = jnp.full((8, queries.shape[0]), NEG, jnp.float32)
    for b in range(2 * half):
        k, at = (k0, b) if b < half else (k1, b - half)
        bias = jnp.where(frames[b] <= limits, 0.0, NEG)
        s = dot_last(k[at * BLOCK : (at + 1) * BLOCK, :], queries) * SCALE2 + bias
        scores[b] = s
        top = jnp.maximum(top, jnp.max(fold(s), axis=0))
    peak = jnp.max(top, axis=0, keepdims=True)
    total = jnp.zeros((8, queries.shape[0]), jnp.float32)
    dots = jnp.zeros((8, queries.shape[0]), jnp.float32)
    for b in range(2 * half):
        v, at = (v0, b) if b < half else (v1, b - half)
        p = jnp.exp2(scores[b] - peak)
        value_dots = dot_last(v[at * BLOCK : (at + 1) * BLOCK, :], grads)
        total = total + jnp.sum(fold(p), axis=0)
        dots = dots + jnp.sum(fold(p * value_dots), axis=0)
    stats[0, pl.ds(head, 1), :] = peak
    stats[1, pl.ds(head, 1), :] = jnp.sum(total, axis=0, keepdims=True)
    stats[2, pl.ds(head, 1), :] = jnp.sum(dots, axis=0, keepdims=True)


def backward_kernel(
    frames, limit, stats, q, do, k0, v0, k1, v1, dq, dk0, dv0, dk1, dv1, lse, rows, kt, weights, grads_s
):
    head = pl.program_id(0)
    half_keys = k0.shape[0]
    half = half_keys // BLOCK

    @pl.when(head == 0)
    def _():
        parts = stats.shape[0]
        peak = stats[0, 0]
        for i in range(1, parts):
            peak = jnp.maximum(peak, stats[i, 0])
        total = jnp.zeros_like(peak)
        dots = jnp.zeros_like(peak)
        for i in range(parts):
            w = jnp.exp2(stats[i, 0] - peak)
            total = total + w * stats[i, 1]
            dots = dots + w * stats[i, 2]
        lse[...] = peak + jnp.log2(total)
        rows[...] = dots / total

    @pl.when(head % GROUP == 0)
    def _():
        kt[:, :half_keys] = k0[...].T
        kt[:, half_keys:] = k1[...].T

    queries = q[...]
    grads = do[...]
    limits = limit[...]
    log_total = lse[pl.ds(head, 1), :]
    row_dots = rows[pl.ds(head, 1), :]
    for b in range(2 * half):
        k, v, at = (k0, v0, b) if b < half else (k1, v1, b - half)
        bias = jnp.where(frames[b] <= limits, -log_total, NEG)
        s = dot_last(k[at * BLOCK : (at + 1) * BLOCK, :], queries)
        p = jnp.exp2(s * SCALE2 + bias)
        value_dots = dot_last(v[at * BLOCK : (at + 1) * BLOCK, :], grads)
        weights[b * BLOCK : (b + 1) * BLOCK, :] = p.astype(jnp.bfloat16)
        grads_s[b * BLOCK : (b + 1) * BLOCK, :] = (p * (value_dots - row_dots)).astype(jnp.bfloat16)
    dq[...] = dot(kt[...], grads_s[...]).T * SCALE
    for at, dk, dv in ((0, dk0, dv0), (half_keys, dk1, dv1)):
        dk_part = dot(grads_s[at : at + half_keys, :], queries)
        dv_part = dot(weights[at : at + half_keys, :], grads)

        @pl.when(head % GROUP == 0)
        def _():
            dk[...] = dk_part
            dv[...] = dv_part

        @pl.when(head % GROUP != 0)
        def _():
            dk[...] += dk_part
            dv[...] += dv_part


def attention_specs(queries, keys, heads):
    scalar = pl.BlockSpec(memory_space=pltpu.SMEM)
    limit = pl.BlockSpec((1, queries), lambda h: (0, 0))
    q = pl.BlockSpec((queries, HEAD_DIM), lambda h: (0, h))
    do = pl.BlockSpec((queries, HEAD_DIM), lambda h: (0, heads + h))
    kv = pl.BlockSpec((keys, HEAD_DIM), lambda h: (0, h // GROUP))
    return scalar, limit, q, do, kv


def forward_stats(frames, limit, both, k0, v0, k1, v1):
    queries, keys = both.shape[0], k0.shape[0]
    heads = both.shape[1] // (2 * HEAD_DIM)
    scalar, lim, q, do, kv = attention_specs(queries, keys, heads)
    work = heads * queries * 2 * keys
    return pl.pallas_call(
        forward_kernel,
        grid=(heads,),
        in_specs=[scalar, lim, q, do, kv, kv, kv, kv],
        out_specs=pl.BlockSpec((3, heads, queries), lambda h: (0, 0, 0)),
        out_shape=jax.ShapeDtypeStruct((3, heads, queries), jnp.float32),
        scratch_shapes=[pltpu.VMEM((2 * keys // BLOCK, BLOCK, queries), jnp.float32)],
        cost_estimate=pl.CostEstimate(
            flops=4 * work * HEAD_DIM, bytes_accessed=4 * both.size, transcendentals=work
        ),
        name="forward_stats",
    )(frames, limit, both, both, k0, v0, k1, v1)


def backward_grads(frames, limit, stats, both, k0, v0, k1, v1):
    queries, keys = both.shape[0], k0.shape[0]
    heads = both.shape[1] // (2 * HEAD_DIM)
    scalar, lim, q, do, kv = attention_specs(queries, keys, heads)
    work = heads * queries * 2 * keys
    key_out = jax.ShapeDtypeStruct(k0.shape, jnp.float32)
    return pl.pallas_call(
        backward_kernel,
        grid=(heads,),
        in_specs=[scalar, lim, pl.BlockSpec(stats.shape, lambda h: (0, 0, 0, 0)), q, do, kv, kv, kv, kv],
        out_specs=[q, kv, kv, kv, kv],
        out_shape=[jax.ShapeDtypeStruct((queries, heads * HEAD_DIM), jnp.float32)] + [key_out] * 4,
        scratch_shapes=[
            pltpu.VMEM((heads, queries), jnp.float32),
            pltpu.VMEM((heads, queries), jnp.float32),
            pltpu.VMEM((HEAD_DIM, 2 * keys), jnp.bfloat16),
            pltpu.VMEM((2 * keys, queries), jnp.bfloat16),
            pltpu.VMEM((2 * keys, queries), jnp.bfloat16),
        ],
        cost_estimate=pl.CostEstimate(
            flops=10 * work * HEAD_DIM, bytes_accessed=8 * both.size, transcendentals=work
        ),
        name="backward_grads",
    )(frames, limit, stats, both, both, k0, v0, k1, v1)


def gather_copies(x, axes):
    count = lax.axis_size(axes)
    copies = jnp.broadcast_to(x[None], (count,) + x.shape)
    return lax.all_to_all(copies, axes, 0, 0, tiled=True)


def swap_z(x):
    return lax.ppermute(x, "vz", [(0, 1), (1, 0)])


def sum_over_heads(partial):
    me = lax.axis_index("head")
    parts = lax.axis_size("head")
    rows = partial.shape[0] // parts
    total = lax.dynamic_slice_in_dim(partial, me * rows, rows, 0)
    for i in range(1, parts):
        piece = lax.dynamic_slice_in_dim(partial, jnp.bitwise_xor(me, i) * rows, rows, 0)
        total = total + lax.ppermute(piece, "head", [(j, j ^ i) for j in range(parts)])
    return total


def shards(text_queries, visual_keys, visual_values, out_grad, query_frame, block_frame, q_weight):
    z = lax.axis_index("vz")
    plane = lax.axis_index(PLANE)
    side = lax.axis_size(PLANE)
    query_rows = text_queries.shape[0]
    blocks = visual_keys.shape[0] // BLOCK
    other_keys, other_values = swap_z(visual_keys), swap_z(visual_values)
    own_frames = lax.dynamic_slice_in_dim(block_frame, (z * side + plane) * blocks, blocks)
    other_frames = lax.dynamic_slice_in_dim(block_frame, ((1 - z) * side + plane) * blocks, blocks)
    frames = jnp.concatenate([own_frames, other_frames])
    queries = query_rows * side
    limit = lax.dynamic_slice_in_dim(query_frame, z * queries, queries)[None]
    own_both = jnp.concatenate([text_queries, out_grad], axis=1)
    both = gather_copies(own_both, PLANE).reshape(queries, own_both.shape[1])
    keys = (visual_keys, visual_values, other_keys, other_values)
    stats = gather_copies(forward_stats(frames, limit, both, *keys), PLANE)
    dq, dk0, dv0, dk1, dv1 = backward_grads(frames, limit, stats, both, *keys)
    key_grad = ((dk0 + swap_z(dk1)) * SCALE).astype(jnp.bfloat16)
    value_grad = (dv0 + swap_z(dv1)).astype(jnp.bfloat16)
    terms = lax.all_to_all(dq.reshape(side, query_rows, -1), PLANE, 0, 0, tiled=True)
    query_grad = jnp.sum(terms, axis=0).astype(jnp.bfloat16)
    query_all = gather_copies(query_grad, VIDEO).reshape(2 * queries, -1)
    partial_text = jnp.dot(query_all, q_weight, preferred_element_type=jnp.float32)
    text_grad = sum_over_heads(partial_text).astype(jnp.bfloat16)
    return (query_grad, key_grad, value_grad, text_grad)


def solution(mesh):
    split = Mesh(
        mesh.devices.reshape(2, 4, 4, mesh.shape["head"]), ("vz", "vx", "vy", "head")
    )
    placed = (
        P(VIDEO, "head"),
        P(VIDEO, "head"),
        P(VIDEO, "head"),
        P(VIDEO, "head"),
        P(),
        P(),
        P("head", VIDEO),
    )
    return jax.shard_map(
        shards,
        mesh=split,
        in_specs=placed,
        out_specs=(P(VIDEO, "head"), P(VIDEO, "head"), P(VIDEO, "head"), P("head", VIDEO)),
        check_vma=False,
    )
```

time: 962 us -> 182 us (0.19)
  waiting for transfers between devices: 460 us -> 60.9 us
  blocking collectives: 240 us -> 41.1 us
  matrix products: 103 us -> 0.71 us
  local copies, waits for them, and re-layouts: 96.6 us -> 6.16 us
  other arithmetic: 46.6 us -> 6.09 us
  Pallas kernels: 0 us -> 34.8 us
  starting transfers between devices: 0.2 us -> 30.7 us
  between operations: 13.9 us -> 0.72 us
    all_gather x4 -> x0, waiting for transfers between devices: 429 us -> none  [the longest x3 349 us: joined_all(): pieces = jax.tree.map(lambda part: lax.all_gather(part, axis), x)]
    psum x1 -> x0, blocking collectives: 188 us -> none  [shards(): query_total = lax.psum(query_sum, VIDEO)]
    dot_general x29 -> x1, matrix products: 103 us -> 0.71 us  [shards(): jnp.dot(query_all, q_weight, preferred_element_type=jnp.float32)]
    all_gather x6 -> x0, blocking collectives: 51.1 us -> none  [joined_all(): pieces = jax.tree.map(lambda part: lax.all_gather(part, axis), x)]
    ppermute x0 -> x7, waiting for transfers between devices: none -> 48.2 us  [the longest x4 42.9 us: swap_z(): return lax.ppermute(x, 'vz', [(0, 1), (1, 0)])]
    all_to_all x0 -> x2, blocking collectives: none -> 41.1 us  [the longest x1 26.8 us: shards(): lax.all_to_all(dq.reshape(side, query_rows, -1), PLANE, 0, 0, tiled=True)]
    unnamed x16 -> x14, local copies, waits for them, and re-layouts: 37.2 us -> 1.37 us
    pallas_call x0 -> x2, Pallas kernels: none -> 34.8 us  [the longest x1 21.4 us: backward_grads(): pl.pallas_call(backward_kernel, grid=(heads,), in_specs=[scalar, lim, pl....]
  transfers between devices with their start and end apart: 5 -> 9, of which waited for: 5 -> 7; matrix products, arithmetic and copies ran while one was open for 3% -> 3% of each run, Pallas kernels for 0% -> 0%
where the time goes in v1:
time: 182 us; the launch traced here: 181 us
  waiting for transfers between devices  60.9 us (33%)
  blocking collectives  41.1 us (23%)
  Pallas kernels  34.8 us (19%)
  starting transfers between devices  30.7 us (17%)
  local copies, waits for them, and re-layouts  6.16 us (3%)
  other arithmetic  6.09 us (3%)
    ppermute x4, waiting for transfers between devices, swap_z(): return lax.ppermute(x, 'vz', [(0, 1), (1, 0)])  42.9 us
    all_to_all x1, blocking collectives, shards(): lax.all_to_all(dq.reshape(side, query_rows, -1), PLANE, 0, 0, tiled=True)  26.8 us
    pallas_call x1, Pallas kernels, backward_grads(): pl.pallas_call(backward_kernel, grid=(heads,), in_specs=[scalar, lim, pl....  21.4 us
    all_to_all x2, starting transfers between devices, gather_copies(): return lax.all_to_all(copies, axes, 0, 0, tiled=True)  16.1 us
    all_to_all x1, blocking collectives, gather_copies(): return lax.all_to_all(copies, axes, 0, 0, tiled=True)  14.3 us
    pallas_call x1, Pallas kernels, forward_stats(): pl.pallas_call(forward_kernel, grid=(heads,), in_specs=[scalar, lim, q, d...  13.4 us
    all_to_all x2, waiting for transfers between devices, gather_copies(): return lax.all_to_all(copies, axes, 0, 0, tiled=True)  12.8 us
    ppermute x3, starting transfers between devices, sum_over_heads(): lax.ppermute(piece, 'head', [(j, j ^ i) for j in range(parts)])  7.81 us
  transfers between devices with their start and end apart: 9, of which 7 were waited for; matrix products, arithmetic and copies ran while one was open for 3% of the time, Pallas kernels for 0%

profile of v1, /device:TPU:1, one launch (start us, length us, event | category | flops | bytes accessed | tf_op | source)
XLA Modules:
  0.0 181.3 jit_solution(626129489593397973)
XLA Ops:
  0.6 0.0 copy-start
  0.6 1.0 pad_maximum_fusion
  1.6 1.6 broadcast_in_dim.9
  3.2 0.0 copy-start.6
  3.2 0.0 copy-start.5
  3.2 0.0 copy-start.4
  3.2 7.7 %all-to-all-start = ((bf16[16,16,4096]{2,1,0:T(8,128)(2,1)}), bf16[16,16,4096]{2,1,0:T(8,128)(2,1)S(1)}, u32[]{:S(2)}, u32[]{:S(2)}) async-start(bf16[16,16,4096]{2,1,0:T(8,128)(2,1)} %broadcast_in_dim.9), calls=%async_computation | async-start | bytes 4194304 | tf_op jit(solution)/shard_map/all_to_all | solution.py:177
  10.9 0.0 copy-done.6
  10.9 3.7 %collective-permute-start = (bf16[512,256]{1,0:T(8,128)(2,1)S(1)}, bf16[512,256]{1,0:T(8,128)(2,1)}, u32[]{:S(2)}, u32[]{:S(2)}) collective-permute-start(bf16[512,256]{1,0:T(8,128)(2,1)S(1)} %copy-done.6), channel_id=1, source_target_pairs={{0,64},{64,0},{1,65},{65,1},{2,66},{66,2},{3,67},{67,3},{4,68},{68... | collective-permute-start | bytes 786440 | tf_op jit(solution)/shard_map/ppermute | solution.py:181
  14.6 0.1 collective-permute-start.1
  14.7 0.0 copy-done.5
  14.7 0.6 dynamic_slice.23
  15.3 0.0 copy-done.4
  15.3 0.1 fusion
  15.4 0.6 pad_add_fusion.frames
  16.0 4.4 %collective-permute-done.k1 = bf16[512,256]{1,0:T(8,128)(2,1)} collective-permute-done((bf16[512,256]{1,0:T(8,128)(2,1)S(1)}, bf16[512,256]{1,0:T(8,128)(2,1)}, u32[]{:S(2)}, u32[]{:S(2)}) %collective-permute-start) | collective-permute-done | bytes 262176 | tf_op jit(solution)/shard_map/ppermute | solution.py:181
  20.4 5.6 %collective-permute-done.1.v1 = bf16[512,256]{1,0:T(8,128)(2,1)} collective-permute-done((bf16[512,256]{1,0:T(8,128)(2,1)}, bf16[512,256]{1,0:T(8,128)(2,1)}, u32[]{:S(2)}, u32[]{:S(2)}) %collective-permute-start.1) | collective-permute-done | bytes 262176 | tf_op jit(solution)/shard_map/ppermute | solution.py:181
  26.1 12.8 %all-to-all-done = bf16[16,16,4096]{2,1,0:T(8,128)(2,1)S(1)} async-done(((bf16[16,16,4096]{2,1,0:T(8,128)(2,1)}), bf16[16,16,4096]{2,1,0:T(8,128)(2,1)S(1)}, u32[]{:S(2)}, u32[]{:S(2)}) %all-to-all-start) | async-done | bytes 2097184 | tf_op jit(solution)/shard_map/all_to_all | solution.py:177
  38.8 0.0 copy-start.1
  38.8 1.3 copy-done.1
  40.1 13.4 %forward_stats.1 = f32[3,16,256]{2,1,0:T(8,128)} custom-call(s32[8]{0:T(128)} %pad_add_fusion.frames, s32[1,256]{1,0:T(1,128)} %bitcast.12, bf16[256,4096]{1,0:T(8,128)(2,1)} %bitcast.6, bf16[256,4096]{1,0:T(8,128)(2,1)} %bitcast.7, bf16[512,256]{1,0:T(8,128)(2,1)} %k0.3, bf16[512,256]{1,0:T(8,128)(2,1)} %v0.3, bf16[512,256]{1,0:T(8,128)(2,1)} %collective-permute-done.k1, ...), custom_call_target="tpu_custom_call" | custom-call | flops 2147483648 | bytes 4194304 | tf_op jit(solution)/shard_map/forward_stats/pallas_call | solution.py:134
  53.5 0.9 broadcast_in_dim.10
  54.4 14.3 %all_to_all.20.stats = f32[16,3,16,256]{3,2,1,0:T(8,128)} all-to-all(f32[16,3,16,256]{3,2,1,0:T(8,128)S(1)} %broadcast_in_dim.10), channel_id=1, replica_groups=mesh['vz'=2,'vx'=4,'vy'=4,'head'=4] {'vx','vy'}, dimensions={0} | all-to-all | bytes 1572864 | tf_op jit(solution)/shard_map/all_to_all | solution.py:177
  68.8 21.4 %backward_grads.1 = (f32[256,2048]{1,0:T(8,128)}, f32[512,256]{1,0:T(8,128)}, f32[512,256]{1,0:T(8,128)}, f32[512,256]{1,0:T(8,128)}, f32[512,256]{1,0:T(8,128)}) custom-call(s32[8]{0:T(128)} %pad_add_fusion.frames, s32[1,256]{1,0:T(1,128)} %bitcast.13, f32[16,3,16,256]{3,2,1,0:T(8,128)} %all_to_all.20.stats, bf16[256,4096]{1,0:T(8,128)(2,1)} %bitcast.8, ...), custom_call_target="tpu_custom_call" | custom-call | flops 5368709120 | bytes 8388608 | tf_op jit(solution)/shard_map/backward_grads/pallas_call | solution.py:154
  90.2 26.8 %all_to_all.21 = f32[16,16,2048]{2,1,0:T(8,128)S(1)} all-to-all(f32[16,16,2048]{2,1,0:T(8,128)} %bitcast.11), channel_id=1, replica_groups=mesh['vz'=2,'vx'=4,'vy'=4,'head'=4] {'vx','vy'}, dimensions={0} | all-to-all | bytes 4194304 | tf_op jit(solution)/shard_map/all_to_all | solution.py:214
  117.0 0.1 reduce_sum.9
  117.1 0.0 copy-start.3
  117.1 1.6 broadcast_in_dim.11
  118.7 0.0 copy-done.3
  118.7 8.4 %all-to-all-start.3 = ((bf16[32,16,2048]{2,1,0:T(8,128)(2,1)}), bf16[32,16,2048]{2,1,0:T(8,128)(2,1)S(1)}, u32[]{:S(2)}, u32[]{:S(2)}) async-start(bf16[32,16,2048]{2,1,0:T(8,128)(2,1)} %broadcast_in_dim.11), calls=%async_computation.3 | async-start | bytes 4194304 | tf_op jit(solution)/shard_map/all_to_all | solution.py:177
  127.1 2.8 %collective-permute-start.3 = (f32[512,256]{1,0:T(8,128)}, f32[512,256]{1,0:T(8,128)}, u32[]{:S(2)}, u32[]{:S(2)}) collective-permute-start(f32[512,256]{1,0:T(8,128)} %get-tuple-element.13), channel_id=1, source_target_pairs={{0,64},{64,0},{1,65},{65,1},{2,66},{66,2},{3,67},{67,3},{4,68},{68... | collective-permute-start | bytes 1572872 | tf_op jit(solution)/shard_map/ppermute | solution.py:181
  129.9 0.2 collective-permute-start.2
  130.1 32.1 %collective-permute-done.3 = f32[512,256]{1,0:T(8,128)} collective-permute-done((f32[512,256]{1,0:T(8,128)}, f32[512,256]{1,0:T(8,128)}, u32[]{:S(2)}, u32[]{:S(2)}) %collective-permute-start.3) | collective-permute-done | bytes 524320 | tf_op jit(solution)/shard_map/ppermute | solution.py:181
  162.3 2.0 %add_convert_fusion = bf16[512,256]{1,0:T(8,128)(2,1)} fusion(f32[512,256]{1,0:T(8,128)} %get-tuple-element.12, f32[512,256]{1,0:T(8,128)} %collective-permute-done.3), kind=kLoop, calls=%fused_computation | loop fusion | flops 262144 | bytes 1310720 | tf_op jit(solution)/shard_map/convert_element_type | solution.py:213
  164.2 0.0 all-to-all-done.3
  164.2 0.0 copy-done
  164.2 0.0 copy-start.2
  164.2 0.7 fusion.1
  165.0 6.1 %collective-permute-start.4 = (f32[128,256]{1,0:T(8,128)S(1)}, f32[128,256]{1,0:T(8,128)S(1)}, u32[]{:S(2)}, u32[]{:S(2)}) collective-permute-start(f32[128,256]{1,0:T(8,128)S(1)} %get-tuple-element.14), channel_id=1, source_target_pairs={{0,1},{1,0},{2,3},{3,2},{4,5},{5,4},{6,7},{7,6},{8,9},{9,8},{10,11... | collective-permute-start | bytes 393224 | tf_op jit(solution)/shard_map/ppermute | solution.py:191
  171.1 0.7 collective-permute-start.5
  171.8 1.0 collective-permute-start.6
  172.8 0.7 collective-permute-done.2
  173.5 0.0 copy-done.2
  173.5 1.8 %multiply_convert_fusion = bf16[512,256]{1,0:T(8,128)(2,1)} fusion(f32[512,256]{1,0:T(8,128)S(1)} %copy-done.2, f32[512,256]{1,0:T(8,128)} %collective-permute-done.2), kind=kLoop, calls=%fused_computation.1 | loop fusion | flops 393216 | bytes 1310720 | tf_op jit(solution)/shard_map/convert_element_type | solution.py:212
  175.3 0.0 collective-permute-done.4
  175.3 1.5 collective-permute-done.5
  176.8 3.8 %collective-permute-done.6 = f32[128,256]{1,0:T(8,128)S(1)} collective-permute-done((f32[128,256]{1,0:T(8,128)S(1)}, f32[128,256]{1,0:T(8,128)S(1)}, u32[]{:S(2)}, u32[]{:S(2)}) %collective-permute-start.6) | collective-permute-done | bytes 131104 | tf_op jit(solution)/shard_map/ppermute | solution.py:191
  180.6 0.7 add_convert_fusion.1
  (1 shorter events, 0.0 us)
Async XLA Ops:
  0.6 163.6 %copy-start = (bf16[2048,256]{1,0:T(8,128)(2,1)S(1)}, bf16[2048,256]{1,0:T(8,128)(2,1)}, u32[]{:S(2)}) copy-start(bf16[2048,256]{1,0:T(8,128)(2,1)} %param.13) | copy-start | bytes 3145732
  3.2 7.7 %copy-start.6 = (bf16[512,256]{1,0:T(8,128)(2,1)S(1)}, bf16[512,256]{1,0:T(8,128)(2,1)}, u32[]{:S(2)}) copy-start(bf16[512,256]{1,0:T(8,128)(2,1)} %k0.3) | copy-start | bytes 786436
  3.2 11.5 %copy-start.5 = (s32[512]{0:T(512)S(1)}, s32[512]{0:T(512)}, u32[]{:S(2)}) copy-start(s32[512]{0:T(512)} %param.11) | copy-start | bytes 6148
  3.2 12.1 %copy-start.4 = (s32[128]{0:T(128)S(1)}, s32[128]{0:T(128)}, u32[]{:S(2)}) copy-start(s32[128]{0:T(128)} %param.12) | copy-start | bytes 1540
  3.2 35.6 %all-to-all-start = ((bf16[16,16,4096]{2,1,0:T(8,128)(2,1)}), bf16[16,16,4096]{2,1,0:T(8,128)(2,1)S(1)}, u32[]{:S(2)}, u32[]{:S(2)}) async-start(bf16[16,16,4096]{2,1,0:T(8,128)(2,1)} %broadcast_in_dim.9), calls=%async_computation | async-start | bytes 4194304 | tf_op jit(solution)/shard_map/all_to_all | solution.py:177
  10.9 9.5 %collective-permute-start = (bf16[512,256]{1,0:T(8,128)(2,1)S(1)}, bf16[512,256]{1,0:T(8,128)(2,1)}, u32[]{:S(2)}, u32[]{:S(2)}) collective-permute-start(bf16[512,256]{1,0:T(8,128)(2,1)S(1)} %copy-done.6), channel_id=1, source_target_pairs={{0,64},{64,0},{1,65},{65,1},{2,66},{66,2},{3,67},{67,3},{4,68},{68... | collective-permute-start | bytes 786440 | tf_op jit(solution)/shard_map/ppermute | solution.py:181
  14.6 11.4 %collective-permute-start.1 = (bf16[512,256]{1,0:T(8,128)(2,1)}, bf16[512,256]{1,0:T(8,128)(2,1)}, u32[]{:S(2)}, u32[]{:S(2)}) collective-permute-start(bf16[512,256]{1,0:T(8,128)(2,1)} %v0.3), channel_id=1, source_target_pairs={{0,64},{64,0},{1,65},{65,1},{2,66},{66,2},{3,67},{67,3},{4,68},{68... | collective-permute-start | bytes 786440 | tf_op jit(solution)/shard_map/ppermute | solution.py:181
  38.8 1.3 copy-start.1
  117.1 1.6 copy-start.3
  118.7 45.5 %all-to-all-start.3 = ((bf16[32,16,2048]{2,1,0:T(8,128)(2,1)}), bf16[32,16,2048]{2,1,0:T(8,128)(2,1)S(1)}, u32[]{:S(2)}, u32[]{:S(2)}) async-start(bf16[32,16,2048]{2,1,0:T(8,128)(2,1)} %broadcast_in_dim.11), calls=%async_computation.3 | async-start | bytes 4194304 | tf_op jit(solution)/shard_map/all_to_all | solution.py:177
  127.1 35.2 %collective-permute-start.3 = (f32[512,256]{1,0:T(8,128)}, f32[512,256]{1,0:T(8,128)}, u32[]{:S(2)}, u32[]{:S(2)}) collective-permute-start(f32[512,256]{1,0:T(8,128)} %get-tuple-element.13), channel_id=1, source_target_pairs={{0,64},{64,0},{1,65},{65,1},{2,66},{66,2},{3,67},{67,3},{4,68},{68... | collective-permute-start | bytes 1572872 | tf_op jit(solution)/shard_map/ppermute | solution.py:181
  129.9 43.6 %collective-permute-start.2 = (f32[512,256]{1,0:T(8,128)}, f32[512,256]{1,0:T(8,128)}, u32[]{:S(2)}, u32[]{:S(2)}) collective-permute-start(f32[512,256]{1,0:T(8,128)} %get-tuple-element.11), channel_id=1, source_target_pairs={{0,64},{64,0},{1,65},{65,1},{2,66},{66,2},{3,67},{67,3},{4,68},{68... | collective-permute-start | bytes 1572872 | tf_op jit(solution)/shard_map/ppermute | solution.py:181
  164.2 9.3 %copy-start.2 = (f32[512,256]{1,0:T(8,128)S(1)}, f32[512,256]{1,0:T(8,128)}, u32[]{:S(2)}) copy-start(f32[512,256]{1,0:T(8,128)} %get-tuple-element.10) | copy-start | bytes 1572868
  165.0 10.3 %collective-permute-start.4 = (f32[128,256]{1,0:T(8,128)S(1)}, f32[128,256]{1,0:T(8,128)S(1)}, u32[]{:S(2)}, u32[]{:S(2)}) collective-permute-start(f32[128,256]{1,0:T(8,128)S(1)} %get-tuple-element.14), channel_id=1, source_target_pairs={{0,1},{1,0},{2,3},{3,2},{4,5},{5,4},{6,7},{7,6},{8,9},{9,8},{10,11... | collective-permute-start | bytes 393224 | tf_op jit(solution)/shard_map/ppermute | solution.py:191
  171.1 5.7 %collective-permute-start.5 = (f32[128,256]{1,0:T(8,128)S(1)}, f32[128,256]{1,0:T(8,128)S(1)}, u32[]{:S(2)}, u32[]{:S(2)}) collective-permute-start(f32[128,256]{1,0:T(8,128)S(1)} %get-tuple-element.16), channel_id=1, source_target_pairs={{0,2},{1,3},{2,0},{3,1},{4,6},{5,7},{6,4},{7,5},{8,10},{9,11},{10,... | collective-permute-start | bytes 393224 | tf_op jit(solution)/shard_map/ppermute | solution.py:191
  171.8 8.8 %collective-permute-start.6 = (f32[128,256]{1,0:T(8,128)S(1)}, f32[128,256]{1,0:T(8,128)S(1)}, u32[]{:S(2)}, u32[]{:S(2)}) collective-permute-start(f32[128,256]{1,0:T(8,128)S(1)} %get-tuple-element.15), channel_id=1, source_target_pairs={{0,3},{1,2},{2,1},{3,0},{4,7},{5,6},{6,5},{7,4},{8,11},{9,10},{10,... | collective-permute-start | bytes 393224 | tf_op jit(solution)/shard_map/ppermute | solution.py:191

commit v2 on v1

--- a/solution.py
+++ b/solution.py
@@ -181,15 +181,26 @@
     return lax.ppermute(x, "vz", [(0, 1), (1, 0)])
 
 
-def sum_over_heads(partial):
-    me = lax.axis_index("head")
-    parts = lax.axis_size("head")
-    rows = partial.shape[0] // parts
-    total = lax.dynamic_slice_in_dim(partial, me * rows, rows, 0)
-    for i in range(1, parts):
-        piece = lax.dynamic_slice_in_dim(partial, jnp.bitwise_xor(me, i) * rows, rows, 0)
-        total = total + lax.ppermute(piece, "head", [(j, j ^ i) for j in range(parts)])
-    return total
+def text_kernel(rows, weight, out):
+    out[0] = dot(rows[...], weight[0])
+
+
+def text_product(rows, weight):
+    count, depth, columns = weight.shape
+    return pl.pallas_call(
+        text_kernel,
+        grid=(count,),
+        in_specs=[
+            pl.BlockSpec(rows.shape, lambda i: (0, 0)),
+            pl.BlockSpec((1, depth, columns), lambda i: (i, 0, 0)),
+        ],
+        out_specs=pl.BlockSpec((1, rows.shape[0], columns), lambda i: (i, 0, 0)),
+        out_shape=jax.ShapeDtypeStruct((count, rows.shape[0], columns), jnp.float32),
+        cost_estimate=pl.CostEstimate(
+            flops=2 * rows.size * count * columns, bytes_accessed=2 * weight.size, transcendentals=0
+        ),
+        name="text_product",
+    )(rows, weight)
 
 
 def shards(text_queries, visual_keys, visual_values, out_grad, query_frame, block_frame, q_weight):
@@ -206,16 +217,25 @@
     limit = lax.dynamic_slice_in_dim(query_frame, z * queries, queries)[None]
     own_both = jnp.concatenate([text_queries, out_grad], axis=1)
     both = gather_copies(own_both, PLANE).reshape(queries, own_both.shape[1])
+    both, other_keys, other_values, q_weight = lax.optimization_barrier(
+        (both, other_keys, other_values, q_weight)
+    )
     keys = (visual_keys, visual_values, other_keys, other_values)
+    weight = lax.all_gather(q_weight, "vy")
     stats = gather_copies(forward_stats(frames, limit, both, *keys), PLANE)
     dq, dk0, dv0, dk1, dv1 = backward_grads(frames, limit, stats, both, *keys)
-    key_grad = ((dk0 + swap_z(dk1)) * SCALE).astype(jnp.bfloat16)
-    value_grad = (dv0 + swap_z(dv1)).astype(jnp.bfloat16)
     terms = lax.all_to_all(dq.reshape(side, query_rows, -1), PLANE, 0, 0, tiled=True)
+    terms, dk1, dv1 = lax.optimization_barrier((terms, swap_z(dk1), swap_z(dv1)))
     query_grad = jnp.sum(terms, axis=0).astype(jnp.bfloat16)
-    query_all = gather_copies(query_grad, VIDEO).reshape(2 * queries, -1)
-    partial_text = jnp.dot(query_all, q_weight, preferred_element_type=jnp.float32)
-    text_grad = sum_over_heads(partial_text).astype(jnp.bfloat16)
+    key_grad = ((dk0 + dk1) * SCALE).astype(jnp.bfloat16)
+    value_grad = (dv0 + dv1).astype(jnp.bfloat16)
+    rows = gather_copies(query_grad, ("vz", "vx"))
+    text = text_product(rows.reshape(-1, rows.shape[-1]), weight)
+    lines, parts = lax.axis_size("vy"), lax.axis_size("head")
+    text = text.reshape(lines * parts, text.shape[1] // parts, text.shape[2])
+    text = lax.all_to_all(text, ("vy", "head"), 0, 0, tiled=True)
+    text = jnp.sum(text.reshape(lines, parts, -1, query_rows, text.shape[2]), axis=1)
+    text_grad = text.transpose(1, 0, 2, 3).reshape(-1, text.shape[3]).astype(jnp.bfloat16)
     return (query_grad, key_grad, value_grad, text_grad)
 
 

time: 182 us -> 179 us (0.984)
  between operations: 0.72 us -> 14.1 us
  blocking collectives: 41.1 us -> 29.8 us
  waiting for transfers between devices: 60.9 us -> 54.5 us
  Pallas kernels: 34.8 us -> 39.6 us
  other arithmetic: 6.09 us -> 2.5 us
  starting transfers between devices: 30.7 us -> 33 us
  local copies, waits for them, and re-layouts: 6.16 us -> 4.01 us
    all_to_all x1 -> x0, blocking collectives: 26.8 us -> none  [shards(): lax.all_to_all(dq.reshape(side, query_rows, -1), PLANE, 0, 0, tiled=True)]
    all_to_all x0 -> x2, starting transfers between devices: none -> 17.7 us  [the longest x1 9.08 us: shards(): text = lax.all_to_all(text, ('vy', 'head'), 0, 0, tiled=True)]
    all_to_all x1 -> x2, blocking collectives: 14.3 us -> 29.8 us  [gather_copies(): return lax.all_to_all(copies, axes, 0, 0, tiled=True)]
    ppermute x4, waiting for transfers between devices: 42.9 us -> 32.9 us  [swap_z(): return lax.ppermute(x, 'vz', [(0, 1), (1, 0)])]
    all_to_all x0 -> x2, waiting for transfers between devices: none -> 8.78 us  [the longest x1 8.69 us: shards(): text = lax.all_to_all(text, ('vy', 'head'), 0, 0, tiled=True)]
    all_to_all x2 -> x1, starting transfers between devices: 16.1 us -> 7.73 us  [gather_copies(): return lax.all_to_all(copies, axes, 0, 0, tiled=True)]
    ppermute x3 -> x0, starting transfers between devices: 7.81 us -> none  [sum_over_heads(): lax.ppermute(piece, 'head', [(j, j ^ i) for j in range(parts)])]
    ppermute x3 -> x0, waiting for transfers between devices: 5.29 us -> none  [sum_over_heads(): lax.ppermute(piece, 'head', [(j, j ^ i) for j in range(parts)])]
  transfers between devices with their start and end apart: 9 -> 8, of which waited for: 7 -> 7; matrix products, arithmetic and copies ran while one was open for 3% -> 2% of each run, Pallas kernels for 0% -> 20%
where the time goes in v2:
time: 179 us; the launch traced here: 178 us
  waiting for transfers between devices  54.5 us (30%)
  Pallas kernels  39.6 us (22%)
  starting transfers between devices  33 us (18%)
  blocking collectives  29.8 us (17%)
  between operations  14.1 us (8%)
  local copies, waits for them, and re-layouts  4.01 us (2%)
  other arithmetic  2.5 us (1%)
    ppermute x4, waiting for transfers between devices, swap_z(): return lax.ppermute(x, 'vz', [(0, 1), (1, 0)])  32.9 us
    all_to_all x2, blocking collectives, gather_copies(): return lax.all_to_all(copies, axes, 0, 0, tiled=True)  29.8 us
    pallas_call x1, Pallas kernels, backward_grads(): pl.pallas_call(backward_kernel, grid=(heads,), in_specs=[scalar, lim, pl....  21.4 us
    pallas_call x1, Pallas kernels, forward_stats(): pl.pallas_call(forward_kernel, grid=(heads,), in_specs=[scalar, lim, q, d...  13.4 us
    all_to_all x1, waiting for transfers between devices, gather_copies(): return lax.all_to_all(copies, axes, 0, 0, tiled=True)  12.8 us
    all_to_all x1, starting transfers between devices, shards(): text = lax.all_to_all(text, ('vy', 'head'), 0, 0, tiled=True)  9.08 us
    all_to_all x1, waiting for transfers between devices, shards(): text = lax.all_to_all(text, ('vy', 'head'), 0, 0, tiled=True)  8.69 us
    all_to_all x1, starting transfers between devices, shards(): lax.all_to_all(dq.reshape(side, query_rows, -1), PLANE, 0, 0, tiled=True)  8.61 us
  transfers between devices with their start and end apart: 8, of which 7 were waited for; matrix products, arithmetic and copies ran while one was open for 2% of the time, Pallas kernels for 20%

profile of v2, /device:TPU:1, one launch (start us, length us, event | category | flops | bytes accessed | tf_op | source)
XLA Modules:
  0.0 177.5 jit_solution(12125587386002908490)
XLA Ops:
  7.2 0.9 pad_maximum_fusion
  8.1 1.6 broadcast_in_dim.9
  9.6 0.0 copy-start.6
  9.6 0.0 copy-start.7
  9.6 0.0 copy-start.5
  9.6 0.0 copy-start.4
  9.6 7.7 %all-to-all-start = ((bf16[16,16,4096]{2,1,0:T(8,128)(2,1)}), bf16[16,16,4096]{2,1,0:T(8,128)(2,1)S(1)}, u32[]{:S(2)}, u32[]{:S(2)}) async-start(bf16[16,16,4096]{2,1,0:T(8,128)(2,1)} %broadcast_in_dim.9), calls=%async_computation | async-start | bytes 4194304 | tf_op jit(solution)/shard_map/all_to_all | solution.py:177
  17.4 0.0 all-gather.3.cloned.1.call-start
  17.4 0.0 copy-done.6
  17.4 3.7 %collective-permute-start = (bf16[512,256]{1,0:T(8,128)(2,1)S(1)}, bf16[512,256]{1,0:T(8,128)(2,1)S(1)}, u32[]{:S(2)}, u32[]{:S(2)}) collective-permute-start(bf16[512,256]{1,0:T(8,128)(2,1)S(1)} %copy-done.6), channel_id=1, source_target_pairs={{0,64},{64,0},{1,65},{65,1},{2,66},{66,2},{3,67},{67,3},{4,68},{68... | collective-permute-start | bytes 786440 | tf_op jit(solution)/shard_map/ppermute | solution.py:181
  21.1 0.0 copy-done.7
  21.1 0.1 collective-permute-start.1
  21.2 5.6 %collective-permute-done.k1 = bf16[512,256]{1,0:T(8,128)(2,1)S(1)} collective-permute-done((bf16[512,256]{1,0:T(8,128)(2,1)S(1)}, bf16[512,256]{1,0:T(8,128)(2,1)S(1)}, u32[]{:S(2)}, u32[]{:S(2)}) %collective-permute-start) | collective-permute-done | bytes 262176 | tf_op jit(solution)/shard_map/ppermute | solution.py:181
  26.8 0.0 copy-start.8
  26.8 5.6 %collective-permute-done.1.v1 = bf16[512,256]{1,0:T(8,128)(2,1)S(1)} collective-permute-done((bf16[512,256]{1,0:T(8,128)(2,1)S(1)}, bf16[512,256]{1,0:T(8,128)(2,1)S(1)}, u32[]{:S(2)}, u32[]{:S(2)}) %collective-permute-start.1) | collective-permute-done | bytes 262176 | tf_op jit(solution)/shard_map/ppermute | solution.py:181
  32.4 0.0 copy-start.9
  32.4 12.8 %all-to-all-done = bf16[16,16,4096]{2,1,0:T(8,128)(2,1)S(1)} async-done(((bf16[16,16,4096]{2,1,0:T(8,128)(2,1)}), bf16[16,16,4096]{2,1,0:T(8,128)(2,1)S(1)}, u32[]{:S(2)}, u32[]{:S(2)}) %all-to-all-start) | async-done | bytes 2097184 | tf_op jit(solution)/shard_map/all_to_all | solution.py:177
  45.3 0.0 copy-start
  45.3 0.0 all-gather.3.cloned.1.call-update
  45.3 0.0 copy-done.5
  45.3 0.8 dynamic_slice.11
  46.1 0.0 copy-done.4
  46.1 0.1 fusion
  46.1 0.6 pad_add_fusion.frames
  46.7 0.0 copy-done.8
  46.7 0.0 copy-done.9
  46.7 0.0 copy-done
  46.7 13.4 %forward_stats.1 = f32[3,16,256]{2,1,0:T(8,128)} custom-call(s32[8]{0:T(128)} %pad_add_fusion.frames, s32[1,256]{1,0:T(1,128)} %bitcast.22, bf16[256,4096]{1,0:T(8,128)(2,1)} %bitcast.14, bf16[256,4096]{1,0:T(8,128)(2,1)} %bitcast.15, bf16[512,256]{1,0:T(8,128)(2,1)} %k0.3, bf16[512,256]{1,0:T(8,128)(2,1)} %v0.3, bf16[512,256]{1,0:T(8,128)(2,1)} %copy-done.8, ...), custom_call_target="tpu_custom_call" | custom-call | flops 2147483648 | bytes 4194304 | tf_op jit(solution)/shard_map/forward_stats/pallas_call | solution.py:134
  60.1 0.9 broadcast_in_dim.10
  61.0 14.3 %all_to_all.25.stats = f32[16,3,16,256]{3,2,1,0:T(8,128)} all-to-all(f32[16,3,16,256]{3,2,1,0:T(8,128)S(1)} %broadcast_in_dim.10), channel_id=1, replica_groups=mesh['vz'=2,'vx'=4,'vy'=4,'head'=4] {'vx','vy'}, dimensions={0} | all-to-all | bytes 1572864 | tf_op jit(solution)/shard_map/all_to_all | solution.py:177
  75.4 21.4 %backward_grads.1 = (f32[256,2048]{1,0:T(8,128)}, f32[512,256]{1,0:T(8,128)}, f32[512,256]{1,0:T(8,128)}, f32[512,256]{1,0:T(8,128)}, f32[512,256]{1,0:T(8,128)}) custom-call(s32[8]{0:T(128)} %pad_add_fusion.frames, s32[1,256]{1,0:T(1,128)} %bitcast.23, f32[16,3,16,256]{3,2,1,0:T(8,128)} %all_to_all.25.stats, bf16[256,4096]{1,0:T(8,128)(2,1)} %bitcast.16, ...), custom_call_target="tpu_custom_call" | custom-call | flops 5368709120 | bytes 8388608 | tf_op jit(solution)/shard_map/backward_grads/pallas_call | solution.py:154
  96.8 8.6 %all-to-all-start.2 = ((f32[16,16,2048]{2,1,0:T(8,128)}), f32[16,16,2048]{2,1,0:T(8,128)S(1)}, u32[]{:S(2)}, u32[]{:S(2)}) async-start(f32[16,16,2048]{2,1,0:T(8,128)} %bitcast.18), calls=%async_computation.2 | async-start | bytes 4194304 | tf_op jit(solution)/shard_map/all_to_all | solution.py:227
  105.4 3.7 %collective-permute-start.2 = (f32[512,256]{1,0:T(8,128)}, f32[512,256]{1,0:T(8,128)S(1)}, u32[]{:S(2)}, u32[]{:S(2)}) collective-permute-start(f32[512,256]{1,0:T(8,128)} %get-tuple-element.20), channel_id=1, source_target_pairs={{0,64},{64,0},{1,65},{65,1},{2,66},{66,2},{3,67},{67,3},{4,68},{68... | collective-permute-start | bytes 1572872 | tf_op jit(solution)/shard_map/ppermute | solution.py:181
  109.1 0.1 collective-permute-start.3
  109.2 10.5 %collective-permute-done.2 = f32[512,256]{1,0:T(8,128)S(1)} collective-permute-done((f32[512,256]{1,0:T(8,128)}, f32[512,256]{1,0:T(8,128)S(1)}, u32[]{:S(2)}, u32[]{:S(2)}) %collective-permute-start.2) | collective-permute-done | bytes 524320 | tf_op jit(solution)/shard_map/ppermute | solution.py:181
  119.6 11.2 %collective-permute-done.3 = f32[512,256]{1,0:T(8,128)S(1)} collective-permute-done((f32[512,256]{1,0:T(8,128)}, f32[512,256]{1,0:T(8,128)S(1)}, u32[]{:S(2)}, u32[]{:S(2)}) %collective-permute-start.3) | collective-permute-done | bytes 524320 | tf_op jit(solution)/shard_map/ppermute | solution.py:181
  130.9 0.1 all-to-all-done.2
  131.0 0.1 reduce_sum.18
  131.1 0.0 copy-start.3
  131.1 15.4 %all_to_all.26 = bf16[8,16,2048]{2,1,0:T(8,128)(2,1)} all-to-all(bf16[8,16,2048]{2,1,0:T(8,128)(2,1)S(1)} %broadcast_in_dim.11), channel_id=1, replica_groups=mesh['vz'=2,'vx'=4,'vy'=4,'head'=4] {'vz','vx'}, dimensions={0} | all-to-all | bytes 1048576 | tf_op jit(solution)/shard_map/all_to_all | solution.py:177
  146.6 0.0 all-gather.3.cloned.1.call-done
  146.6 0.0 copy-start.1
  146.6 0.0 copy-start.2
  146.6 4.7 %text_product.1 = f32[4,128,256]{2,1,0:T(8,128)} custom-call(bf16[128,2048]{1,0:T(8,128)(2,1)} %bitcast.13, bf16[4,2048,256]{2,1,0:T(8,128)(2,1)} %bitcast.11), custom_call_target="tpu_custom_call" | custom-call | flops 536870912 | bytes 4194304 | tf_op jit(solution)/shard_map/text_product/pallas_call | solution.py:190
  151.3 0.0 copy-done.3
  151.3 9.1 %all-to-all-start.4 = ((f32[16,32,256]{2,1,0:T(8,128)}), f32[16,32,256]{2,1,0:T(8,128)S(1)}, u32[]{:S(2)}, u32[]{:S(2)}) async-start(f32[16,32,256]{2,1,0:T(8,128)} %bitcast.12), calls=%async_computation.4 | async-start | bytes 1048576 | tf_op jit(solution)/shard_map/all_to_all | solution.py:236
  160.4 0.0 copy-done.1
  160.4 0.0 copy-done.2
  160.4 0.9 add_convert_fusion
  161.3 8.7 %all-to-all-done.4 = f32[16,32,256]{2,1,0:T(8,128)S(1)} async-done(((f32[16,32,256]{2,1,0:T(8,128)}), f32[16,32,256]{2,1,0:T(8,128)S(1)}, u32[]{:S(2)}, u32[]{:S(2)}) %all-to-all-start.4) | async-done | bytes 524320 | tf_op jit(solution)/shard_map/all_to_all | solution.py:236
  170.0 0.6 copy.11
  (2 shorter events, 0.1 us)
Async XLA Ops:
  9.6 7.8 %copy-start.6 = (bf16[512,256]{1,0:T(8,128)(2,1)S(1)}, bf16[512,256]{1,0:T(8,128)(2,1)}, u32[]{:S(2)}) copy-start(bf16[512,256]{1,0:T(8,128)(2,1)} %k0.3) | copy-start | bytes 786436
  9.6 11.5 %copy-start.7 = (bf16[512,256]{1,0:T(8,128)(2,1)S(1)}, bf16[512,256]{1,0:T(8,128)(2,1)}, u32[]{:S(2)}) copy-start(bf16[512,256]{1,0:T(8,128)(2,1)} %v0.3) | copy-start | bytes 786436
  9.6 35.7 %copy-start.5 = (s32[512]{0:T(512)S(1)}, s32[512]{0:T(512)}, u32[]{:S(2)}) copy-start(s32[512]{0:T(512)} %param.11) | copy-start | bytes 6148
  9.6 36.4 %copy-start.4 = (s32[128]{0:T(128)S(1)}, s32[128]{0:T(128)}, u32[]{:S(2)}) copy-start(s32[128]{0:T(128)} %param.12) | copy-start | bytes 1540
  9.6 35.6 %all-to-all-start = ((bf16[16,16,4096]{2,1,0:T(8,128)(2,1)}), bf16[16,16,4096]{2,1,0:T(8,128)(2,1)S(1)}, u32[]{:S(2)}, u32[]{:S(2)}) async-start(bf16[16,16,4096]{2,1,0:T(8,128)(2,1)} %broadcast_in_dim.9), calls=%async_computation | async-start | bytes 4194304 | tf_op jit(solution)/shard_map/all_to_all | solution.py:177
  17.4 129.2 %all-gather.3.cloned.1.call-start = ((), (), s32[]{:S(2)}) async-start(), calls=%async_computation.5 | async-start | bytes 5242880 | tf_op jit(solution)/shard_map/all_gather | solution.py:224
  17.4 9.4 %collective-permute-start = (bf16[512,256]{1,0:T(8,128)(2,1)S(1)}, bf16[512,256]{1,0:T(8,128)(2,1)S(1)}, u32[]{:S(2)}, u32[]{:S(2)}) collective-permute-start(bf16[512,256]{1,0:T(8,128)(2,1)S(1)} %copy-done.6), channel_id=1, source_target_pairs={{0,64},{64,0},{1,65},{65,1},{2,66},{66,2},{3,67},{67,3},{4,68},{68... | collective-permute-start | bytes 786440 | tf_op jit(solution)/shard_map/ppermute | solution.py:181
  21.1 11.3 %collective-permute-start.1 = (bf16[512,256]{1,0:T(8,128)(2,1)S(1)}, bf16[512,256]{1,0:T(8,128)(2,1)S(1)}, u32[]{:S(2)}, u32[]{:S(2)}) collective-permute-start(bf16[512,256]{1,0:T(8,128)(2,1)S(1)} %copy-done.7), channel_id=1, source_target_pairs={{0,64},{64,0},{1,65},{65,1},{2,66},{66,2},{3,67},{67,3},{4,68},{68... | collective-permute-start | bytes 786440 | tf_op jit(solution)/shard_map/ppermute | solution.py:181
  26.8 19.9 %copy-start.8 = (bf16[512,256]{1,0:T(8,128)(2,1)}, bf16[512,256]{1,0:T(8,128)(2,1)S(1)}, u32[]{:S(2)}) copy-start(bf16[512,256]{1,0:T(8,128)(2,1)S(1)} %collective-permute-done.k1) | copy-start | bytes 786436
  32.4 14.3 %copy-start.9 = (bf16[512,256]{1,0:T(8,128)(2,1)}, bf16[512,256]{1,0:T(8,128)(2,1)S(1)}, u32[]{:S(2)}) copy-start(bf16[512,256]{1,0:T(8,128)(2,1)S(1)} %collective-permute-done.1.v1) | copy-start | bytes 786436
  45.3 1.5 copy-start
  96.8 34.2 %all-to-all-start.2 = ((f32[16,16,2048]{2,1,0:T(8,128)}), f32[16,16,2048]{2,1,0:T(8,128)S(1)}, u32[]{:S(2)}, u32[]{:S(2)}) async-start(f32[16,16,2048]{2,1,0:T(8,128)} %bitcast.18), calls=%async_computation.2 | async-start | bytes 4194304 | tf_op jit(solution)/shard_map/all_to_all | solution.py:227
  105.4 14.2 %collective-permute-start.2 = (f32[512,256]{1,0:T(8,128)}, f32[512,256]{1,0:T(8,128)S(1)}, u32[]{:S(2)}, u32[]{:S(2)}) collective-permute-start(f32[512,256]{1,0:T(8,128)} %get-tuple-element.20), channel_id=1, source_target_pairs={{0,64},{64,0},{1,65},{65,1},{2,66},{66,2},{3,67},{67,3},{4,68},{68... | collective-permute-start | bytes 1572872 | tf_op jit(solution)/shard_map/ppermute | solution.py:181
  109.1 21.8 %collective-permute-start.3 = (f32[512,256]{1,0:T(8,128)}, f32[512,256]{1,0:T(8,128)S(1)}, u32[]{:S(2)}, u32[]{:S(2)}) collective-permute-start(f32[512,256]{1,0:T(8,128)} %get-tuple-element.21), channel_id=1, source_target_pairs={{0,64},{64,0},{1,65},{65,1},{2,66},{66,2},{3,67},{67,3},{4,68},{68... | collective-permute-start | bytes 1572872 | tf_op jit(solution)/shard_map/ppermute | solution.py:181
  131.1 20.2 %copy-start.3 = (bf16[16,2048]{1,0:T(8,128)(2,1)}, bf16[16,2048]{1,0:T(8,128)(2,1)S(1)}, u32[]{:S(2)}) copy-start(bf16[16,2048]{1,0:T(8,128)(2,1)S(1)} %reduce_sum.18) | copy-start | bytes 196612
  146.6 13.8 %copy-start.1 = (f32[512,256]{1,0:T(8,128)S(1)}, f32[512,256]{1,0:T(8,128)}, u32[]{:S(2)}) copy-start(f32[512,256]{1,0:T(8,128)} %get-tuple-element.23) | copy-start | bytes 1572868
  146.6 13.8 %copy-start.2 = (f32[512,256]{1,0:T(8,128)S(1)}, f32[512,256]{1,0:T(8,128)}, u32[]{:S(2)}) copy-start(f32[512,256]{1,0:T(8,128)} %get-tuple-element.25) | copy-start | bytes 1572868
  151.3 18.7 %all-to-all-start.4 = ((f32[16,32,256]{2,1,0:T(8,128)}), f32[16,32,256]{2,1,0:T(8,128)S(1)}, u32[]{:S(2)}, u32[]{:S(2)}) async-start(f32[16,32,256]{2,1,0:T(8,128)} %bitcast.12), calls=%async_computation.4 | async-start | bytes 1048576 | tf_op jit(solution)/shard_map/all_to_all | solution.py:236
Sparse Core Ops, SparseCore 0:
  45.4 58.4 all-gather.2

commit v3 on v2

v3 whole, which is shorter than its diff:
```python
import functools
import math

import jax
import jax.numpy as jnp
from jax import lax
from jax.experimental import pallas as pl
from jax.experimental.pallas import tpu as pltpu
from jax.sharding import Mesh
from jax.sharding import PartitionSpec as P

HEADS = 64
KV_HEADS = 8
GROUP = HEADS // KV_HEADS
HEAD_DIM = 128
BLOCK = 128
VIDEO = ("vz", "vx", "vy")
PLANE = ("vx", "vy")
SCALE = HEAD_DIM ** -0.5
SCALE2 = SCALE * math.log2(math.e)
NEG = -1.0e30
CONTRACT_LAST = (((1,), (1,)), ((), ()))


def dot_last(a, b):
    return lax.dot_general(a, b, CONTRACT_LAST, preferred_element_type=jnp.float32)


def dot(a, b):
    return jnp.dot(a, b, preferred_element_type=jnp.float32)


def fold(x):
    return x.reshape(x.shape[0] // 8, 8, x.shape[1])


def pieces_of(x):
    high = x.astype(jnp.bfloat16).astype(jnp.float32)
    rest = x - high
    middle = rest.astype(jnp.bfloat16).astype(jnp.float32)
    return [high, middle, rest - middle]


def local_kernel(frames, limit, q, do, k0, v0, k1, v1, sums, stats, scores, dots, weights, grads_s, kt):
    step = pl.program_id(0)
    heads = stats.shape[1]
    half_keys = k0.shape[0]
    half = half_keys // BLOCK

    @pl.when(jnp.logical_and(step % GROUP == 0, step < heads))
    def _():
        kt[:, :half_keys] = k0[...].T
        kt[:, half_keys:] = k1[...].T

    @pl.when(step < heads)
    def _():
        queries = q[...]
        grads = do[...]
        limits = limit[...]
        top = jnp.full((8, queries.shape[0]), NEG, jnp.float32)
        for b in range(2 * half):
            k, at = (k0, b) if b < half else (k1, b - half)
            bias = jnp.where(frames[b] <= limits, 0.0, NEG)
            s = dot_last(k[at * BLOCK : (at + 1) * BLOCK, :], queries) * SCALE2 + bias
            scores[b] = s
            top = jnp.maximum(top, jnp.max(fold(s), axis=0))
        peak = jnp.max(top, axis=0, keepdims=True)
        total = jnp.zeros((8, queries.shape[0]), jnp.float32)
        moment = jnp.zeros((8, queries.shape[0]), jnp.float32)
        for b in range(2 * half):
            v, at = (v0, b) if b < half else (v1, b - half)
            p = jnp.exp2(scores[b] - peak)
            value_dots = dot_last(v[at * BLOCK : (at + 1) * BLOCK, :], grads)
            scores[b] = p
            dots[b] = value_dots
            weights[b * BLOCK : (b + 1) * BLOCK, :] = p.astype(jnp.bfloat16)
            total = total + jnp.sum(fold(p), axis=0)
            moment = moment + jnp.sum(fold(p * value_dots), axis=0)
        total = jnp.sum(total, axis=0, keepdims=True)
        share = 1.0 / total
        mean = jnp.sum(moment, axis=0, keepdims=True) * share
        for b in range(2 * half):
            grads_s[b * BLOCK : (b + 1) * BLOCK, :] = (scores[b] * (dots[b] - mean)).astype(jnp.bfloat16)
        sums[:, :HEAD_DIM] = (dot(kt[...], grads_s[...]) * share).T.astype(jnp.bfloat16)
        sums[:, HEAD_DIM:] = (dot(kt[...], weights[...]) * share).T.astype(jnp.bfloat16)
        stats[0, pl.ds(step, 1), :] = peak + jnp.log2(total)
        stats[1, pl.ds(step, 1), :] = mean

    @pl.when(step == heads)
    def _():
        rows = pieces_of(stats[0]) + pieces_of(stats[1])
        rows = jnp.concatenate(rows + [jnp.zeros_like(rows[0])] * 2, axis=0)
        sums[:, :HEAD_DIM] = rows.T.astype(jnp.bfloat16)
        sums[:, HEAD_DIM:] = jnp.zeros_like(sums[:, HEAD_DIM:])


def keys_kernel(frames, limit, lse, rows, q, do, k0, v0, k1, v1, dk0, dv0, dk1, dv1, weights, grads_s):
    head = pl.program_id(0)
    half_keys = k0.shape[0]
    half = half_keys // BLOCK
    queries = q[...]
    grads = do[...]
    limits = limit[...]
    log_total = lse[pl.ds(head, 1), :]
    row_dots = rows[pl.ds(head, 1), :]
    for b in range(2 * half):
        k, v, at = (k0, v0, b) if b < half else (k1, v1, b - half)
        bias = jnp.where(frames[b] <= limits, -log_total, NEG)
        s = dot_last(k[at * BLOCK : (at + 1) * BLOCK, :], queries)
        p = jnp.exp2(s * SCALE2 + bias)
        value_dots = dot_last(v[at * BLOCK : (at + 1) * BLOCK, :], grads)
        weights[b * BLOCK : (b + 1) * BLOCK, :] = p.astype(jnp.bfloat16)
        grads_s[b * BLOCK : (b + 1) * BLOCK, :] = (p * (value_dots - row_dots)).astype(jnp.bfloat16)
    for at, dk, dv in ((0, dk0, dv0), (half_keys, dk1, dv1)):
        dk_part = dot(grads_s[at : at + half_keys, :], queries)
        dv_part = dot(weights[at : at + half_keys, :], grads)

        @pl.when(head % GROUP == 0)
        def _():
            dk[...] = dk_part
            dv[...] = dv_part

        @pl.when(head % GROUP != 0)
        def _():
            dk[...] += dk_part
            dv[...] += dv_part


def combine_kernel(terms, out):
    sources = terms.shape[0]
    heads = out.shape[2] // HEAD_DIM
    tops, means = [], []
    for i in range(sources):
        t = terms[i, :, 2 * heads * HEAD_DIM : (2 * heads + 1) * HEAD_DIM].astype(jnp.float32)
        t = t + pltpu.roll(t, HEAD_DIM - heads, 1) + pltpu.roll(t, HEAD_DIM - 2 * heads, 1)
        tops.append(t)
        means.append(pltpu.roll(t, HEAD_DIM - 3 * heads, 1))
    peak = functools.reduce(jnp.maximum, tops)
    shares = [jnp.exp2(t - peak) for t in tops]
    total = sum(shares)
    row_dots = sum(w * m for w, m in zip(shares, means)) / total
    scale = SCALE / total
    factors = [w * scale for w in shares]
    shifts = [f * (m - row_dots) for f, m in zip(factors, means)]
    for j in range(heads):
        result = jnp.zeros((terms.shape[1], HEAD_DIM), jnp.float32)
        for part, scales in enumerate((factors, shifts)):
            at = (2 * j + part) * HEAD_DIM
            for i in range(sources):
                result = result + scales[i][:, j : j + 1] * terms[i, :, at : at + HEAD_DIM].astype(jnp.float32)
        for i in range(out.shape[0]):
            out[i, :, j * HEAD_DIM : (j + 1) * HEAD_DIM] = result.astype(jnp.bfloat16)


def attention_specs(queries, keys, heads):
    scalar = pl.BlockSpec(memory_space=pltpu.SMEM)
    limit = pl.BlockSpec((1, queries), lambda h: (0, 0))
    q = pl.BlockSpec((queries, HEAD_DIM), lambda h: (0, h))
    do = pl.BlockSpec((queries, HEAD_DIM), lambda h: (0, heads + h))
    kv = pl.BlockSpec((keys, HEAD_DIM), lambda h: (0, h // GROUP))
    return scalar, limit, q, do, kv


def local_sums(frames, limit, both, k0, v0, k1, v1):
    queries, keys = both.shape[0], k0.shape[0]
    heads = both.shape[1] // (2 * HEAD_DIM)
    last = heads - 1
    scalar = pl.BlockSpec(memory_space=pltpu.SMEM)
    lim = pl.BlockSpec((1, queries), lambda h: (0, 0))
    q = pl.BlockSpec((queries, HEAD_DIM), lambda h: (0, jnp.minimum(h, last)))
    do = pl.BlockSpec((queries, HEAD_DIM), lambda h: (0, heads + jnp.minimum(h, last)))
    kv = pl.BlockSpec((keys, HEAD_DIM), lambda h: (0, jnp.minimum(h, last) // GROUP))
    work = heads * queries * 2 * keys
    blocks = 2 * keys // BLOCK
    return pl.pallas_call(
        local_kernel,
        grid=(heads + 1,),
        in_specs=[scalar, lim, q, do, kv, kv, kv, kv],
        out_specs=[
            pl.BlockSpec((queries, 2 * HEAD_DIM), lambda h: (0, h)),
            pl.BlockSpec((2, heads, queries), lambda h: (0, 0, 0)),
        ],
        out_shape=[
            jax.ShapeDtypeStruct((queries, (heads + 1) * 2 * HEAD_DIM), jnp.bfloat16),
            jax.ShapeDtypeStruct((2, heads, queries), jnp.float32),
        ],
        scratch_shapes=[
            pltpu.VMEM((blocks, BLOCK, queries), jnp.float32),
            pltpu.VMEM((blocks, BLOCK, queries), jnp.float32),
            pltpu.VMEM((2 * keys, queries), jnp.bfloat16),
            pltpu.VMEM((2 * keys, queries), jnp.bfloat16),
            pltpu.VMEM((HEAD_DIM, 2 * keys), jnp.bfloat16),
        ],
        cost_estimate=pl.CostEstimate(
            flops=8 * work * HEAD_DIM, bytes_accessed=8 * both.size, transcendentals=work
        ),
        name="local_sums",
    )(frames, limit, both, both, k0, v0, k1, v1)


def key_value_grads(frames, limit, lse, row_dots, both, k0, v0, k1, v1):
    queries, keys = both.shape[0], k0.shape[0]
    heads = both.shape[1] // (2 * HEAD_DIM)
    scalar, lim, q, do, kv = attention_specs(queries, keys, heads)
    work = heads * queries * 2 * keys
    row = pl.BlockSpec((heads, queries), lambda h: (0, 0))
    return pl.pallas_call(
        keys_kernel,
        grid=(heads,),
        in_specs=[scalar, lim, row, row, q, do, kv, kv, kv, kv],
        out_specs=[kv, kv, kv, kv],
        out_shape=[jax.ShapeDtypeStruct(k0.shape, jnp.float32)] * 4,
        scratch_shapes=[
            pltpu.VMEM((2 * keys, queries), jnp.bfloat16),
            pltpu.VMEM((2 * keys, queries), jnp.bfloat16),
        ],
        cost_estimate=pl.CostEstimate(
            flops=8 * work * HEAD_DIM, bytes_accessed=8 * both.size, transcendentals=work
        ),
        name="key_value_grads",
    )(frames, limit, lse, row_dots, both, both, k0, v0, k1, v1)


def combine_terms(terms, heads, copies):
    vmem = pl.BlockSpec(memory_space=pltpu.VMEM)
    return pl.pallas_call(
        combine_kernel,
        in_specs=[vmem],
        out_specs=vmem,
        out_shape=jax.ShapeDtypeStruct((copies, terms.shape[1], heads * HEAD_DIM), jnp.bfloat16),
        cost_estimate=pl.CostEstimate(
            flops=2 * terms.size, bytes_accessed=2 * terms.size, transcendentals=0
        ),
        name="combine_terms",
    )(terms)


def merge_stats(stats, axis):
    size = lax.axis_size(axis)
    parts = [stats]
    for shift in range(1, size):
        parts.append(lax.ppermute(stats, axis, [(i, (i + shift) % size) for i in range(size)]))
    peak = functools.reduce(jnp.maximum, [p[0] for p in parts])
    shares = [jnp.exp2(p[0] - peak) for p in parts]
    total = sum(shares)
    mean = sum(w * p[1] for w, p in zip(shares, parts)) / total
    return jnp.stack([peak + jnp.log2(total), mean])


def gather_copies(x, axes):
    count = lax.axis_size(axes)
    copies = jnp.broadcast_to(x[None], (count,) + x.shape)
    return lax.all_to_all(copies, axes, 0, 0, tiled=True)


def swap_z(x):
    return lax.ppermute(x, "vz", [(0, 1), (1, 0)])


def line_pieces(x):
    half = x.shape[0] // 2
    ahead = [(i, (i + 1) % 4) for i in range(4)]
    back = [(i, (i + 3) % 4) for i in range(4)]
    below = lax.ppermute(x, "vy", ahead)
    above = lax.ppermute(x, "vy", back)
    return x, below, above, lax.ppermute(below[:half], "vy", ahead), lax.ppermute(above[half:], "vy", back)


def text_kernel(line, rows, own, below, above, far0, far1, out):
    count = out.shape[0]
    half = far0.shape[0]
    me = line[0]
    out[me] = dot(rows[...], own[...])
    out[lax.rem(me + count - 1, count)] = dot(rows[...], below[...])
    out[lax.rem(me + 1, count)] = dot(rows[...], above[...])
    out[lax.rem(me + 2, count)] = dot(rows[:, :half], far0[...]) + dot(rows[:, half:], far1[...])


def text_product(rows, weights):
    count = lax.axis_size("vy")
    depth, columns = weights[0].shape
    vmem = pl.BlockSpec(memory_space=pltpu.VMEM)
    return pl.pallas_call(
        text_kernel,
        in_specs=[pl.BlockSpec(memory_space=pltpu.SMEM)] + [vmem] * 6,
        out_specs=vmem,
        out_shape=jax.ShapeDtypeStruct((count, rows.shape[0], columns), jnp.float32),
        cost_estimate=pl.CostEstimate(
            flops=2 * rows.size * count * columns, bytes_accessed=2 * count * depth * columns, transcendentals=0
        ),
        name="text_product",
    )(lax.axis_index("vy").reshape(1), rows, *weights)


def shards(text_queries, visual_keys, visual_values, out_grad, query_frame, block_frame, q_weight):
    z = lax.axis_index("vz")
    plane = lax.axis_index(PLANE)
    side = lax.axis_size(PLANE)
    query_rows = text_queries.shape[0]
    blocks = visual_keys.shape[0] // BLOCK
    other_keys, other_values = swap_z(visual_keys), swap_z(visual_values)
    own_frames = lax.dynamic_slice_in_dim(block_frame, (z * side + plane) * blocks, blocks)
    other_frames = lax.dynamic_slice_in_dim(block_frame, ((1 - z) * side + plane) * blocks, blocks)
    frames = jnp.concatenate([own_frames, other_frames])
    queries = query_rows * side
    limit = lax.dynamic_slice_in_dim(query_frame, z * queries, queries)[None]
    own_both = jnp.concatenate([text_queries, out_grad], axis=1)
    both = gather_copies(own_both, PLANE).reshape(queries, own_both.shape[1])
    both, other_keys, other_values, q_weight = lax.optimization_barrier(
        (both, other_keys, other_values, q_weight)
    )
    keys = (visual_keys, visual_values, other_keys, other_values)
    sums, stats = local_sums(frames, limit, both, *keys)
    terms = lax.all_to_all(sums.reshape(side, query_rows, -1), PLANE, 0, 0, tiled=True)
    lse, row_dots = merge_stats(merge_stats(stats, "vx"), "vy")
    dk0, dv0, dk1, dv1 = key_value_grads(frames, limit, lse, row_dots, both, *keys)
    copies = combine_terms(terms, text_queries.shape[1] // HEAD_DIM, lax.axis_size(("vz", "vx")))
    rows = lax.all_to_all(copies, ("vz", "vx"), 0, 0, tiled=True)
    query_grad = copies[0]
    key_grad = ((dk0 + swap_z(dk1)) * SCALE).astype(jnp.bfloat16)
    value_grad = (dv0 + swap_z(dv1)).astype(jnp.bfloat16)
    weights = line_pieces(q_weight)
    text = text_product(rows.reshape(-1, rows.shape[-1]), weights)
    lines, parts = lax.axis_size("vy"), lax.axis_size("head")
    text = text.reshape(lines * parts, text.shape[1] // parts, text.shape[2])
    text = lax.all_to_all(text, ("vy", "head"), 0, 0, tiled=True)
    text = jnp.sum(text.reshape(lines, parts, -1, query_rows, text.shape[2]), axis=1)
    text_grad = text.transpose(1, 0, 2, 3).reshape(-1, text.shape[3]).astype(jnp.bfloat16)
    return (query_grad, key_grad, value_grad, text_grad)


def solution(mesh):
    split = Mesh(
        mesh.devices.reshape(2, 4, 4, mesh.shape["head"]), ("vz", "vx", "vy", "head")
    )
    placed = (
        P(VIDEO, "head"),
        P(VIDEO, "head"),
        P(VIDEO, "head"),
        P(VIDEO, "head"),
        P(),
        P(),
        P("head", VIDEO),
    )
    return jax.shard_map(
        shards,
        mesh=split,
        in_specs=placed,
        out_specs=(P(VIDEO, "head"), P(VIDEO, "head"), P(VIDEO, "head"), P("head", VIDEO)),
        check_vma=False,
    )
```

time: 179 us -> 177 us (0.989)
  blocking collectives: 29.8 us -> 0 us
  starting transfers between devices: 33 us -> 49.9 us
  between operations: 14.1 us -> 0.74 us
  Pallas kernels: 39.6 us -> 47.6 us
  local copies, waits for them, and re-layouts: 4.01 us -> 10.8 us
  waiting for transfers between devices: 54.5 us -> 60.5 us
  other arithmetic: 2.5 us -> 6.62 us
    all_to_all x2 -> x0, blocking collectives: 29.8 us -> none  [gather_copies(): return lax.all_to_all(copies, axes, 0, 0, tiled=True)]
    ppermute x0 -> x10, waiting for transfers between devices: none -> 24.3 us  [the longest x6 24.3 us: merge_stats(): lax.ppermute(stats, axis, [(i, (i + shift) % size) for i in range(size)])]
    ppermute x4, waiting for transfers between devices: 32.9 us -> 9.89 us  [swap_z(): return lax.ppermute(x, 'vz', [(0, 1), (1, 0)])]
    ppermute x0 -> x10, starting transfers between devices: none -> 12 us  [the longest x6 6.63 us: merge_stats(): lax.ppermute(stats, axis, [(i, (i + shift) % size) for i in range(size)])]
    pallas_call x3 -> x4, Pallas kernels: 39.6 us -> 47.6 us  [the longest x1 20.9 us: local_sums(): pl.pallas_call(local_kernel, grid=(heads + 1,), in_specs=[scalar, lim, q,...]
    all_to_all x1 -> x2, waiting for transfers between devices: 0.08 us -> 7.06 us  [the longest x1 7.06 us: shards(): rows = lax.all_to_all(copies, ('vz', 'vx'), 0, 0, tiled=True)]
    unnamed x20 -> x24, local copies, waits for them, and re-layouts: 0.04 us -> 3.54 us
    all_to_all x1, starting transfers between devices: 9.08 us -> 12 us  [shards(): text = lax.all_to_all(text, ('vy', 'head'), 0, 0, tiled=True)]
  transfers between devices with their start and end apart: 8 -> 18, of which waited for: 7 -> 9; matrix products, arithmetic and copies ran while one was open for 2% -> 6% of each run, Pallas kernels for 20% -> 15%
where the time goes in v3:
time: 177 us; the launch traced here: 176 us
  waiting for transfers between devices  60.5 us (34%)
  starting transfers between devices  49.9 us (28%)
  Pallas kernels  47.6 us (27%)
  local copies, waits for them, and re-layouts  10.8 us (6%)
  other arithmetic  6.62 us (4%)
    ppermute x6, waiting for transfers between devices, merge_stats(): lax.ppermute(stats, axis, [(i, (i + shift) % size) for i in range(size)])  24.3 us
    pallas_call x1, Pallas kernels, local_sums(): pl.pallas_call(local_kernel, grid=(heads + 1,), in_specs=[scalar, lim, q,...  20.9 us
    pallas_call x1, Pallas kernels, key_value_grads(): pl.pallas_call(keys_kernel, grid=(heads,), in_specs=[scalar, lim, row, ro...  19.1 us
    all_to_all x1, waiting for transfers between devices, gather_copies(): return lax.all_to_all(copies, axes, 0, 0, tiled=True)  12.9 us
    all_to_all x1, starting transfers between devices, shards(): text = lax.all_to_all(text, ('vy', 'head'), 0, 0, tiled=True)  12 us
    ppermute x4, waiting for transfers between devices, swap_z(): return lax.ppermute(x, 'vz', [(0, 1), (1, 0)])  9.89 us
    all_to_all x1, starting transfers between devices, gather_copies(): return lax.all_to_all(copies, axes, 0, 0, tiled=True)  7.73 us
    ppermute x4, starting transfers between devices, swap_z(): return lax.ppermute(x, 'vz', [(0, 1), (1, 0)])  7.34 us
  transfers between devices with their start and end apart: 18, of which 9 were waited for; matrix products, arithmetic and copies ran while one was open for 6% of the time, Pallas kernels for 15%

profile of v3, /device:TPU:1, one launch (start us, length us, event | category | flops | bytes accessed | tf_op | source)
XLA Modules:
  0.0 176.2 jit_solution(1551208352241227156)
XLA Ops:
  0.6 0.9 pad_maximum_fusion
  1.5 1.6 broadcast_in_dim.10
  3.1 7.7 %all-to-all-start = ((bf16[16,16,4096]{2,1,0:T(8,128)(2,1)}), bf16[16,16,4096]{2,1,0:T(8,128)(2,1)S(1)}, u32[]{:S(2)}, u32[]{:S(2)}) async-start(bf16[16,16,4096]{2,1,0:T(8,128)(2,1)} %broadcast_in_dim.10), calls=%async_computation | async-start | bytes 4194304 | tf_op jit(solution)/shard_map/all_to_all | solution.py:253
  10.8 0.0 copy-done.8
  10.9 3.7 %collective-permute-start = (bf16[512,256]{1,0:T(8,128)(2,1)S(1)}, bf16[512,256]{1,0:T(8,128)(2,1)S(1)}, u32[]{:S(2)}, u32[]{:S(2)}) collective-permute-start(bf16[512,256]{1,0:T(8,128)(2,1)S(1)} %copy-done.8), channel_id=1, source_target_pairs={{0,64},{64,0},{1,65},{65,1},{2,66},{66,2},{3,67},{67,3},{4,68},{68... | collective-permute-start | bytes 786440 | tf_op jit(solution)/shard_map/ppermute | solution.py:257
  14.5 0.0 copy-done.9
  14.5 0.1 collective-permute-start.1
  14.6 0.0 copy-done.7
  14.6 0.7 dynamic_slice.11
  15.3 0.0 copy-done.6
  15.3 0.1 fusion.20
  15.4 0.6 pad_add_fusion.frames
  16.0 4.3 %collective-permute-done.k1 = bf16[512,256]{1,0:T(8,128)(2,1)S(1)} collective-permute-done((bf16[512,256]{1,0:T(8,128)(2,1)S(1)}, bf16[512,256]{1,0:T(8,128)(2,1)S(1)}, u32[]{:S(2)}, u32[]{:S(2)}) %collective-permute-start) | collective-permute-done | bytes 262176 | tf_op jit(solution)/shard_map/ppermute | solution.py:257
  20.2 5.6 %collective-permute-done.1.v1 = bf16[512,256]{1,0:T(8,128)(2,1)S(1)} collective-permute-done((bf16[512,256]{1,0:T(8,128)(2,1)S(1)}, bf16[512,256]{1,0:T(8,128)(2,1)S(1)}, u32[]{:S(2)}, u32[]{:S(2)}) %collective-permute-start.1) | collective-permute-done | bytes 262176 | tf_op jit(solution)/shard_map/ppermute | solution.py:257
  25.9 12.9 %all-to-all-done = bf16[16,16,4096]{2,1,0:T(8,128)(2,1)S(1)} async-done(((bf16[16,16,4096]{2,1,0:T(8,128)(2,1)}), bf16[16,16,4096]{2,1,0:T(8,128)(2,1)S(1)}, u32[]{:S(2)}, u32[]{:S(2)}) %all-to-all-start) | async-done | bytes 2097184 | tf_op jit(solution)/shard_map/all_to_all | solution.py:253
  38.7 0.0 copy-done.10
  38.7 0.0 copy-done.11
  38.7 1.3 copy-done.2
  40.0 20.9 %local_sums.1 = (bf16[256,4352]{1,0:T(8,128)(2,1)}, f32[2,16,256]{2,1,0:T(8,128)}) custom-call(s32[8]{0:T(128)} %pad_add_fusion.frames, s32[1,256]{1,0:T(1,128)} %bitcast.167, bf16[256,4096]{1,0:T(8,128)(2,1)} %bitcast.158, bf16[256,4096]{1,0:T(8,128)(2,1)} %bitcast.159, bf16[512,256]{1,0:T(8,128)(2,1)} %k0.3, bf16[512,256]{1,0:T(8,128)(2,1)} %v0.3, ...), custom_call_target="tpu_custom_call" | custom-call | flops 4294967296 | bytes 8388608 | tf_op jit(solution)/shard_map/local_sums/pallas_call | solution.py:175
  61.0 3.9 %all-to-all-start.1 = ((bf16[16,16,4352]{2,1,0:T(8,128)(2,1)}), bf16[16,16,4352]{2,1,0:T(8,128)(2,1)S(1)}, u32[]{:S(2)}, u32[]{:S(2)}) async-start(bf16[16,16,4352]{2,1,0:T(8,128)(2,1)} %bitcast.157), calls=%async_computation.1 | async-start | bytes 4456448 | tf_op jit(solution)/shard_map/all_to_all | solution.py:314
  64.8 0.0 copy-done.5
  64.9 2.6 %collective-permute-start.4 = (f32[2,16,256]{2,1,0:T(8,128)S(1)}, f32[2,16,256]{2,1,0:T(8,128)S(1)}, u32[]{:S(2)}, u32[]{:S(2)}) collective-permute-start(f32[2,16,256]{2,1,0:T(8,128)S(1)} %copy-done.5), channel_id=1, source_target_pairs={{0,48},{16,0},{32,16},{48,32},{1,49},{17,1},{33,17},{49,33},{2,50}... | collective-permute-start | bytes 98312 | tf_op jit(solution)/shard_map/ppermute | solution.py:242
  67.5 0.6 collective-permute-start.3
  68.1 0.6 collective-permute-start.2
  68.7 21.0 %collective-permute-done.4 = f32[2,16,256]{2,1,0:T(8,128)S(1)} collective-permute-done((f32[2,16,256]{2,1,0:T(8,128)S(1)}, f32[2,16,256]{2,1,0:T(8,128)S(1)}, u32[]{:S(2)}, u32[]{:S(2)}) %collective-permute-start.4) | collective-permute-done | bytes 32800 | tf_op jit(solution)/shard_map/ppermute | solution.py:242
  89.7 2.0 %collective-permute-done.3 = f32[2,16,256]{2,1,0:T(8,128)S(1)} collective-permute-done((f32[2,16,256]{2,1,0:T(8,128)S(1)}, f32[2,16,256]{2,1,0:T(8,128)S(1)}, u32[]{:S(2)}, u32[]{:S(2)}) %collective-permute-start.3) | collective-permute-done | bytes 32800 | tf_op jit(solution)/shard_map/ppermute | solution.py:242
  91.7 0.0 collective-permute-done.2
  91.7 1.0 collective-permute-start.7
  92.7 1.9 %collective-permute-start.6 = (f32[2,16,256]{2,1,0:T(8,128)S(1)}, f32[2,16,256]{2,1,0:T(8,128)S(1)}, u32[]{:S(2)}, u32[]{:S(2)}) collective-permute-start(f32[2,16,256]{2,1,0:T(8,128)S(1)} %pad_maximum_fusion.1), channel_id=1, source_target_pairs={{0,8},{4,12},{8,0},{12,4},{1,9},{5,13},{9,1},{13,5},{2,10},{6,14},... | collective-permute-start | bytes 98312 | tf_op jit(solution)/shard_map/ppermute | solution.py:242
  94.5 0.0 collective-permute-start.5
  94.5 0.8 collective-permute-start.10
  95.3 1.9 %collective-permute-start.11 = (bf16[2048,256]{1,0:T(8,128)(2,1)}, bf16[2048,256]{1,0:T(8,128)(2,1)}, u32[]{:S(2)}, u32[]{:S(2)}) collective-permute-start(bf16[2048,256]{1,0:T(8,128)(2,1)} %own), channel_id=1, source_target_pairs={{0,12},{4,0},{8,4},{12,8},{1,13},{5,1},{9,5},{13,9},{2,14},{6,2},{... | collective-permute-start | bytes 3145736 | tf_op jit(solution)/shard_map/ppermute | solution.py:265
  97.3 0.0 collective-permute-done.7
  97.3 0.4 collective-permute-done.6
  97.7 0.9 collective-permute-done.5
  98.5 0.7 fusion.2
  99.2 0.6 multiply_add_fusion.lse
  99.8 19.1 %key_value_grads.1 = (f32[512,256]{1,0:T(8,128)}, f32[512,256]{1,0:T(8,128)}, f32[512,256]{1,0:T(8,128)}, f32[512,256]{1,0:T(8,128)}) custom-call(s32[8]{0:T(128)} %pad_add_fusion.frames, s32[1,256]{1,0:T(1,128)} %bitcast.168, f32[16,256]{1,0:T(8,128)} %multiply_add_fusion.lse, f32[16,256]{1,0:T(8,128)} %get-tuple-element.24.rows, ...), custom_call_target="tpu_custom_call" | custom-call | flops 4294967296 | bytes 8388608 | tf_op jit(solution)/shard_map/key_value_grads/pallas_call | solution.py:207
  118.9 3.5 %collective-permute-start.8 = (f32[512,256]{1,0:T(8,128)}, f32[512,256]{1,0:T(8,128)}, u32[]{:S(2)}, u32[]{:S(2)}) collective-permute-start(f32[512,256]{1,0:T(8,128)} %get-tuple-element.20), channel_id=1, source_target_pairs={{0,64},{64,0},{1,65},{65,1},{2,66},{66,2},{3,67},{67,3},{4,68},{68... | collective-permute-start | bytes 1572872 | tf_op jit(solution)/shard_map/ppermute | solution.py:257
  122.4 0.0 collective-permute-done.10.below
  122.4 0.9 slice.88
  123.3 0.0 collective-permute-start.12
  123.3 0.0 collective-permute-done.11.above
  123.3 1.9 %slice.89 = bf16[1024,256]{1,0:T(8,128)(2,1)} slice(bf16[2048,256]{1,0:T(8,128)(2,1)} %collective-permute-done.11.above), slice={[1024:2048], [0:256]} | slice | bytes 1048576 | tf_op jit(solution)/shard_map/slice | solution.py:266
  125.2 2.7 %collective-permute-start.13 = (bf16[1024,256]{1,0:T(8,128)(2,1)}, bf16[1024,256]{1,0:T(8,128)(2,1)}, u32[]{:S(2)}, u32[]{:S(2)}) collective-permute-start(bf16[1024,256]{1,0:T(8,128)(2,1)} %slice.89), channel_id=1, source_target_pairs={{0,12},{4,0},{8,4},{12,8},{1,13},{5,1},{9,5},{13,9},{2,14},{6,2},{... | collective-permute-start | bytes 1572872 | tf_op jit(solution)/shard_map/ppermute | solution.py:266
  127.9 0.0 collective-permute-start.9
  127.9 0.0 all-to-all-done.1.terms
  127.9 1.4 copy-done
  129.3 3.7 %combine_terms.1 = bf16[8,16,2048]{2,1,0:T(8,128)(2,1)} custom-call(bf16[16,16,4352]{2,1,0:T(8,128)(2,1)} %copy-done), custom_call_target="tpu_custom_call" | custom-call | flops 2228224 | bytes 2228224 | tf_op jit(solution)/shard_map/combine_terms/pallas_call | solution.py:226
  133.1 0.0 copy-done.1
  133.1 7.0 %all-to-all-start.2 = ((bf16[8,16,2048]{2,1,0:T(8,128)(2,1)}), bf16[8,16,2048]{2,1,0:T(8,128)(2,1)S(1)}, u32[]{:S(2)}, u32[]{:S(2)}) async-start(bf16[8,16,2048]{2,1,0:T(8,128)(2,1)} %combine_terms.1), calls=%async_computation.2 | async-start | bytes 1048576 | tf_op jit(solution)/shard_map/all_to_all | solution.py:318
  140.1 0.0 collective-permute-done.8
  140.1 2.0 %multiply_convert_fusion = bf16[512,256]{1,0:T(8,128)(2,1)} fusion(f32[512,256]{1,0:T(8,128)} %get-tuple-element.19, f32[512,256]{1,0:T(8,128)} %collective-permute-done.8), kind=kLoop, calls=%fused_computation.1 | loop fusion | flops 393216 | bytes 1310720 | tf_op jit(solution)/shard_map/convert_element_type | solution.py:320
  142.0 0.0 collective-permute-done.12.far0
  142.0 0.0 collective-permute-done.13.far1
  142.0 7.1 %all-to-all-done.2 = bf16[8,16,2048]{2,1,0:T(8,128)(2,1)S(1)} async-done(((bf16[8,16,2048]{2,1,0:T(8,128)(2,1)}), bf16[8,16,2048]{2,1,0:T(8,128)(2,1)S(1)}, u32[]{:S(2)}, u32[]{:S(2)}) %all-to-all-start.2) | async-done | bytes 524320 | tf_op jit(solution)/shard_map/all_to_all | solution.py:318
  149.1 0.8 copy-done.3
  149.9 3.9 %text_product.1 = f32[4,128,256]{2,1,0:T(8,128)} custom-call(s32[1]{0:T(128)} %bitcast.18.line, bf16[128,2048]{1,0:T(8,128)(2,1)} %bitcast.163, bf16[2048,256]{1,0:T(8,128)(2,1)} %own, bf16[2048,256]{1,0:T(8,128)(2,1)} %copy-done.1, bf16[2048,256]{1,0:T(8,128)(2,1)} %collective-permute-done.11.above, bf16[1024,256]{1,0:T(8,128)(2,1)} %collective-permute-done.12.far0, ...), custom_call_target="tpu_custom_call" | custom-call | flops 536870912 | bytes 4194304 | tf_op jit(solution)/shard_map/text_product/pallas_call | solution.py:283
  153.8 12.0 %all-to-all-start.3 = ((f32[16,32,256]{2,1,0:T(8,128)}), f32[16,32,256]{2,1,0:T(8,128)S(1)}, u32[]{:S(2)}, u32[]{:S(2)}) async-start(f32[16,32,256]{2,1,0:T(8,128)} %bitcast.164), calls=%async_computation.3 | async-start | bytes 1048576 | tf_op jit(solution)/shard_map/all_to_all | solution.py:326
  165.8 0.0 collective-permute-done.9
  165.8 1.8 %add_convert_fusion = bf16[512,256]{1,0:T(8,128)(2,1)} fusion(f32[512,256]{1,0:T(8,128)S(1)} %copy-done.4, f32[512,256]{1,0:T(8,128)} %collective-permute-done.9), kind=kLoop, calls=%fused_computation | loop fusion | flops 262144 | bytes 1310720 | tf_op jit(solution)/shard_map/convert_element_type | solution.py:321
  167.6 1.5 slice_bitcast_fusion
  169.1 6.4 %all-to-all-done.3 = f32[16,32,256]{2,1,0:T(8,128)S(1)} async-done(((f32[16,32,256]{2,1,0:T(8,128)}), f32[16,32,256]{2,1,0:T(8,128)S(1)}, u32[]{:S(2)}, u32[]{:S(2)}) %all-to-all-start.3) | async-done | bytes 524320 | tf_op jit(solution)/shard_map/all_to_all | solution.py:326
  175.5 0.6 copy.11
  (16 shorter events, 0.1 us)
Async XLA Ops:
  3.1 7.7 %copy-start.8 = (bf16[512,256]{1,0:T(8,128)(2,1)S(1)}, bf16[512,256]{1,0:T(8,128)(2,1)}, u32[]{:S(2)}) copy-start(bf16[512,256]{1,0:T(8,128)(2,1)} %k0.3) | copy-start | bytes 786436
  3.1 11.4 %copy-start.9 = (bf16[512,256]{1,0:T(8,128)(2,1)S(1)}, bf16[512,256]{1,0:T(8,128)(2,1)}, u32[]{:S(2)}) copy-start(bf16[512,256]{1,0:T(8,128)(2,1)} %v0.3) | copy-start | bytes 786436
  3.1 11.5 %copy-start.7 = (s32[512]{0:T(512)S(1)}, s32[512]{0:T(512)}, u32[]{:S(2)}) copy-start(s32[512]{0:T(512)} %param.11) | copy-start | bytes 6148
  3.1 12.2 %copy-start.6 = (s32[128]{0:T(128)S(1)}, s32[128]{0:T(128)}, u32[]{:S(2)}) copy-start(s32[128]{0:T(128)} %param.12) | copy-start | bytes 1540
  3.1 35.6 %all-to-all-start = ((bf16[16,16,4096]{2,1,0:T(8,128)(2,1)}), bf16[16,16,4096]{2,1,0:T(8,128)(2,1)S(1)}, u32[]{:S(2)}, u32[]{:S(2)}) async-start(bf16[16,16,4096]{2,1,0:T(8,128)(2,1)} %broadcast_in_dim.10), calls=%async_computation | async-start | bytes 4194304 | tf_op jit(solution)/shard_map/all_to_all | solution.py:253
  10.9 9.4 %collective-permute-start = (bf16[512,256]{1,0:T(8,128)(2,1)S(1)}, bf16[512,256]{1,0:T(8,128)(2,1)S(1)}, u32[]{:S(2)}, u32[]{:S(2)}) collective-permute-start(bf16[512,256]{1,0:T(8,128)(2,1)S(1)} %copy-done.8), channel_id=1, source_target_pairs={{0,64},{64,0},{1,65},{65,1},{2,66},{66,2},{3,67},{67,3},{4,68},{68... | collective-permute-start | bytes 786440 | tf_op jit(solution)/shard_map/ppermute | solution.py:257
  14.5 11.3 %collective-permute-start.1 = (bf16[512,256]{1,0:T(8,128)(2,1)S(1)}, bf16[512,256]{1,0:T(8,128)(2,1)S(1)}, u32[]{:S(2)}, u32[]{:S(2)}) collective-permute-start(bf16[512,256]{1,0:T(8,128)(2,1)S(1)} %copy-done.9), channel_id=1, source_target_pairs={{0,64},{64,0},{1,65},{65,1},{2,66},{66,2},{3,67},{67,3},{4,68},{68... | collective-permute-start | bytes 786440 | tf_op jit(solution)/shard_map/ppermute | solution.py:257
  20.2 18.5 %copy-start.10 = (bf16[512,256]{1,0:T(8,128)(2,1)}, bf16[512,256]{1,0:T(8,128)(2,1)S(1)}, u32[]{:S(2)}) copy-start(bf16[512,256]{1,0:T(8,128)(2,1)S(1)} %collective-permute-done.k1) | copy-start | bytes 786436
  25.9 12.9 %copy-start.11 = (bf16[512,256]{1,0:T(8,128)(2,1)}, bf16[512,256]{1,0:T(8,128)(2,1)S(1)}, u32[]{:S(2)}) copy-start(bf16[512,256]{1,0:T(8,128)(2,1)S(1)} %collective-permute-done.1.v1) | copy-start | bytes 786436
  38.7 1.3 copy-start.2
  61.0 3.9 %copy-start.5 = (f32[2,16,256]{2,1,0:T(8,128)S(1)}, f32[2,16,256]{2,1,0:T(8,128)}, u32[]{:S(2)}) copy-start(f32[2,16,256]{2,1,0:T(8,128)} %get-tuple-element.18) | copy-start | bytes 98308
  61.0 66.9 %all-to-all-start.1 = ((bf16[16,16,4352]{2,1,0:T(8,128)(2,1)}), bf16[16,16,4352]{2,1,0:T(8,128)(2,1)S(1)}, u32[]{:S(2)}, u32[]{:S(2)}) async-start(bf16[16,16,4352]{2,1,0:T(8,128)(2,1)} %bitcast.157), calls=%async_computation.1 | async-start | bytes 4456448 | tf_op jit(solution)/shard_map/all_to_all | solution.py:314
  64.9 24.8 %collective-permute-start.4 = (f32[2,16,256]{2,1,0:T(8,128)S(1)}, f32[2,16,256]{2,1,0:T(8,128)S(1)}, u32[]{:S(2)}, u32[]{:S(2)}) collective-permute-start(f32[2,16,256]{2,1,0:T(8,128)S(1)} %copy-done.5), channel_id=1, source_target_pairs={{0,48},{16,0},{32,16},{48,32},{1,49},{17,1},{33,17},{49,33},{2,50}... | collective-permute-start | bytes 98312 | tf_op jit(solution)/shard_map/ppermute | solution.py:242
  67.5 24.2 %collective-permute-start.3 = (f32[2,16,256]{2,1,0:T(8,128)S(1)}, f32[2,16,256]{2,1,0:T(8,128)S(1)}, u32[]{:S(2)}, u32[]{:S(2)}) collective-permute-start(f32[2,16,256]{2,1,0:T(8,128)S(1)} %copy-done.5), channel_id=1, source_target_pairs={{0,32},{16,48},{32,0},{48,16},{1,33},{17,49},{33,1},{49,17},{2,34}... | collective-permute-start | bytes 98312 | tf_op jit(solution)/shard_map/ppermute | solution.py:242
  68.1 23.6 %collective-permute-start.2 = (f32[2,16,256]{2,1,0:T(8,128)S(1)}, f32[2,16,256]{2,1,0:T(8,128)S(1)}, u32[]{:S(2)}, u32[]{:S(2)}) collective-permute-start(f32[2,16,256]{2,1,0:T(8,128)S(1)} %copy-done.5), channel_id=1, source_target_pairs={{0,16},{16,32},{32,48},{48,0},{1,17},{17,33},{33,49},{49,1},{2,18}... | collective-permute-start | bytes 98312 | tf_op jit(solution)/shard_map/ppermute | solution.py:242
  91.7 5.5 %collective-permute-start.7 = (f32[2,16,256]{2,1,0:T(8,128)S(1)}, f32[2,16,256]{2,1,0:T(8,128)S(1)}, u32[]{:S(2)}, u32[]{:S(2)}) collective-permute-start(f32[2,16,256]{2,1,0:T(8,128)S(1)} %pad_maximum_fusion.1), channel_id=1, source_target_pairs={{0,12},{4,0},{8,4},{12,8},{1,13},{5,1},{9,5},{13,9},{2,14},{6,2},{... | collective-permute-start | bytes 98312 | tf_op jit(solution)/shard_map/ppermute | solution.py:242
  92.7 5.0 %collective-permute-start.6 = (f32[2,16,256]{2,1,0:T(8,128)S(1)}, f32[2,16,256]{2,1,0:T(8,128)S(1)}, u32[]{:S(2)}, u32[]{:S(2)}) collective-permute-start(f32[2,16,256]{2,1,0:T(8,128)S(1)} %pad_maximum_fusion.1), channel_id=1, source_target_pairs={{0,8},{4,12},{8,0},{12,4},{1,9},{5,13},{9,1},{13,5},{2,10},{6,14},... | collective-permute-start | bytes 98312 | tf_op jit(solution)/shard_map/ppermute | solution.py:242
  94.5 4.0 %collective-permute-start.5 = (f32[2,16,256]{2,1,0:T(8,128)S(1)}, f32[2,16,256]{2,1,0:T(8,128)S(1)}, u32[]{:S(2)}, u32[]{:S(2)}) collective-permute-start(f32[2,16,256]{2,1,0:T(8,128)S(1)} %pad_maximum_fusion.1), channel_id=1, source_target_pairs={{0,4},{4,8},{8,12},{12,0},{1,5},{5,9},{9,13},{13,1},{2,6},{6,10},{... | collective-permute-start | bytes 98312 | tf_op jit(solution)/shard_map/ppermute | solution.py:242
  94.5 27.9 %collective-permute-start.10 = (bf16[2048,256]{1,0:T(8,128)(2,1)}, bf16[2048,256]{1,0:T(8,128)(2,1)S(1)}, u32[]{:S(2)}, u32[]{:S(2)}) collective-permute-start(bf16[2048,256]{1,0:T(8,128)(2,1)} %own), channel_id=1, source_target_pairs={{0,4},{4,8},{8,12},{12,0},{1,5},{5,9},{9,13},{13,1},{2,6},{6,10},{... | collective-permute-start | bytes 3145736 | tf_op jit(solution)/shard_map/ppermute | solution.py:264
  95.3 28.0 %collective-permute-start.11 = (bf16[2048,256]{1,0:T(8,128)(2,1)}, bf16[2048,256]{1,0:T(8,128)(2,1)}, u32[]{:S(2)}, u32[]{:S(2)}) collective-permute-start(bf16[2048,256]{1,0:T(8,128)(2,1)} %own), channel_id=1, source_target_pairs={{0,12},{4,0},{8,4},{12,8},{1,13},{5,1},{9,5},{13,9},{2,14},{6,2},{... | collective-permute-start | bytes 3145736 | tf_op jit(solution)/shard_map/ppermute | solution.py:265
  118.9 21.2 %collective-permute-start.8 = (f32[512,256]{1,0:T(8,128)}, f32[512,256]{1,0:T(8,128)}, u32[]{:S(2)}, u32[]{:S(2)}) collective-permute-start(f32[512,256]{1,0:T(8,128)} %get-tuple-element.20), channel_id=1, source_target_pairs={{0,64},{64,0},{1,65},{65,1},{2,66},{66,2},{3,67},{67,3},{4,68},{68... | collective-permute-start | bytes 1572872 | tf_op jit(solution)/shard_map/ppermute | solution.py:257
  122.4 10.7 %copy-start.1 = (bf16[2048,256]{1,0:T(8,128)(2,1)}, bf16[2048,256]{1,0:T(8,128)(2,1)S(1)}, u32[]{:S(2)}) copy-start(bf16[2048,256]{1,0:T(8,128)(2,1)S(1)} %collective-permute-done.10.below) | copy-start | bytes 3145732
  123.3 18.7 %collective-permute-start.12 = (bf16[1024,256]{1,0:T(8,128)(2,1)}, bf16[1024,256]{1,0:T(8,128)(2,1)}, u32[]{:S(2)}, u32[]{:S(2)}) collective-permute-start(bf16[1024,256]{1,0:T(8,128)(2,1)} %slice.88), channel_id=1, source_target_pairs={{0,4},{4,8},{8,12},{12,0},{1,5},{5,9},{9,13},{13,1},{2,6},{6,10},{... | collective-permute-start | bytes 1572872 | tf_op jit(solution)/shard_map/ppermute | solution.py:266
  125.2 16.8 %collective-permute-start.13 = (bf16[1024,256]{1,0:T(8,128)(2,1)}, bf16[1024,256]{1,0:T(8,128)(2,1)}, u32[]{:S(2)}, u32[]{:S(2)}) collective-permute-start(bf16[1024,256]{1,0:T(8,128)(2,1)} %slice.89), channel_id=1, source_target_pairs={{0,12},{4,0},{8,4},{12,8},{1,13},{5,1},{9,5},{13,9},{2,14},{6,2},{... | collective-permute-start | bytes 1572872 | tf_op jit(solution)/shard_map/ppermute | solution.py:266
  127.9 37.9 %collective-permute-start.9 = (f32[512,256]{1,0:T(8,128)}, f32[512,256]{1,0:T(8,128)}, u32[]{:S(2)}, u32[]{:S(2)}) collective-permute-start(f32[512,256]{1,0:T(8,128)} %get-tuple-element.22), channel_id=1, source_target_pairs={{0,64},{64,0},{1,65},{65,1},{2,66},{66,2},{3,67},{67,3},{4,68},{68... | collective-permute-start | bytes 1572872 | tf_op jit(solution)/shard_map/ppermute | solution.py:257
  127.9 1.4 copy-start
  133.1 16.0 %all-to-all-start.2 = ((bf16[8,16,2048]{2,1,0:T(8,128)(2,1)}), bf16[8,16,2048]{2,1,0:T(8,128)(2,1)S(1)}, u32[]{:S(2)}, u32[]{:S(2)}) async-start(bf16[8,16,2048]{2,1,0:T(8,128)(2,1)} %combine_terms.1), calls=%async_computation.2 | async-start | bytes 1048576 | tf_op jit(solution)/shard_map/all_to_all | solution.py:318
  149.1 0.8 copy-start.3
  149.9 15.9 %copy-start.4 = (f32[512,256]{1,0:T(8,128)S(1)}, f32[512,256]{1,0:T(8,128)}, u32[]{:S(2)}) copy-start(f32[512,256]{1,0:T(8,128)} %get-tuple-element.21) | copy-start | bytes 1572868
  153.8 21.7 %all-to-all-start.3 = ((f32[16,32,256]{2,1,0:T(8,128)}), f32[16,32,256]{2,1,0:T(8,128)S(1)}, u32[]{:S(2)}, u32[]{:S(2)}) async-start(f32[16,32,256]{2,1,0:T(8,128)} %bitcast.164), calls=%async_computation.3 | async-start | bytes 1048576 | tf_op jit(solution)/shard_map/all_to_all | solution.py:326

commit v4 on v2

v4 whole, which is shorter than its diff:
```python
import functools
import math

import jax
import jax.numpy as jnp
from jax import lax
from jax.experimental import pallas as pl
from jax.experimental.pallas import tpu as pltpu
from jax.sharding import Mesh
from jax.sharding import PartitionSpec as P

HEADS = 64
KV_HEADS = 8
GROUP = HEADS // KV_HEADS
HEAD_DIM = 128
BLOCK = 128
VIDEO = ("vz", "vx", "vy")
PLANE = ("vx", "vy")
SCALE = HEAD_DIM ** -0.5
SCALE2 = SCALE * math.log2(math.e)
NEG = -1.0e30
PER_STEP = 4
CONTRACT_LAST = (((1,), (1,)), ((), ()))


def dot_last(a, b):
    return lax.dot_general(a, b, CONTRACT_LAST, preferred_element_type=jnp.float32)


def dot(a, b):
    return jnp.dot(a, b, preferred_element_type=jnp.float32)


def fold(x):
    return x.reshape(x.shape[0] // 8, 8, x.shape[1])


def head_columns(j):
    return slice(j * HEAD_DIM, (j + 1) * HEAD_DIM)


def key_bias(frames, first, limits, seen):
    rows = [jnp.where(frames[first + b] <= limits, seen, NEG) for b in range(frames.shape[0] // 2)]
    return jnp.concatenate([jnp.broadcast_to(r, (BLOCK, r.shape[1])) for r in rows], axis=0)


def forward_kernel(frames, limit, q, do, k0, v0, k1, v1, stats, scores):
    step = pl.program_id(0)
    limits = limit[...]
    half_keys = k0.shape[0]
    half = half_keys // BLOCK
    for j in range(PER_STEP):
        queries = q[:, head_columns(j)]
        grads = do[:, head_columns(j)]
        tops = []
        for at, k in ((0, k0), (1, k1)):
            s = dot_last(k[...], queries) * SCALE2 + key_bias(frames, at * half, limits, 0.0)
            scores[j, at] = s
            tops.append(jnp.max(fold(s), axis=0))
        peak = jnp.max(jnp.maximum(*tops), axis=0, keepdims=True)
        total = jnp.zeros((8, queries.shape[0]), jnp.float32)
        moment = jnp.zeros((8, queries.shape[0]), jnp.float32)
        for at, v in ((0, v0), (1, v1)):
            p = jnp.exp2(scores[j, at] - peak)
            value_dots = dot_last(v[...], grads)
            total = total + jnp.sum(fold(p), axis=0)
            moment = moment + jnp.sum(fold(p * value_dots), axis=0)
        total = jnp.sum(total, axis=0, keepdims=True)
        head = step * PER_STEP + j
        stats[0, pl.ds(head, 1), :] = peak + jnp.log2(total)
        stats[1, pl.ds(head, 1), :] = jnp.sum(moment, axis=0, keepdims=True) / total


def merge_stats(stats):
    sources = stats.shape[0]
    peak = functools.reduce(jnp.maximum, [stats[i, 0] for i in range(sources)])
    shares = [jnp.exp2(stats[i, 0] - peak) for i in range(sources)]
    total = sum(shares)
    row_dots = sum(w * stats[i, 1] for i, w in enumerate(shares)) / total
    return peak + jnp.log2(total), row_dots


def query_kernel(frames, limit, stats, q, do, k0, v0, k1, v1, dq, bias, columns):
    step = pl.program_id(0)
    heads = stats.shape[2]
    half_keys = k0.shape[0]

    @pl.when(step == 0)
    def _():
        limits = limit[...]
        for at in range(2):
            half = half_keys // BLOCK
            bias[:, at * half_keys : (at + 1) * half_keys] = key_bias(frames, at * half, limits, 0.0).T
        log_total, row_dots = merge_stats(stats)
        filler = jnp.zeros((HEAD_DIM - 2 * PER_STEP, log_total.shape[1]), jnp.float32)
        for i in range(heads // PER_STEP):
            rows = slice(i * PER_STEP, (i + 1) * PER_STEP)
            columns[i] = jnp.concatenate([log_total[rows], row_dots[rows], filler], axis=0).T

    for j in range(PER_STEP):
        queries = q[:, head_columns(j)]
        grads = do[:, head_columns(j)]
        log_total = columns[step, :, j : j + 1]
        row_dots = columns[step, :, PER_STEP + j : PER_STEP + j + 1]
        result = jnp.zeros((queries.shape[0], HEAD_DIM), jnp.float32)
        for at, k, v in ((0, k0, v0), (half_keys, k1, v1)):
            s = dot_last(queries, k[...]) * SCALE2 + bias[:, at : at + half_keys]
            p = jnp.exp2(s - log_total)
            value_dots = dot_last(grads, v[...])
            result = result + dot((p * (value_dots - row_dots)).astype(jnp.bfloat16), k[...])
        dq[:, head_columns(j)] = result * SCALE


def keys_kernel(frames, limit, stats, q, do, k0, v0, k1, v1, dk0, dv0, dk1, dv1, lse, rows):
    step = pl.program_id(0)
    limits = limit[...]
    half = k0.shape[0] // BLOCK

    @pl.when(step == 0)
    def _():
        lse[...], rows[...] = merge_stats(stats)

    first = step % (GROUP // PER_STEP) == 0
    for at, k, v, dk, dv in ((0, k0, v0, dk0, dv0), (half, k1, v1, dk1, dv1)):
        dk_part = jnp.zeros(dk.shape, jnp.float32)
        dv_part = jnp.zeros(dv.shape, jnp.float32)
        for j in range(PER_STEP):
            queries = q[:, head_columns(j)]
            grads = do[:, head_columns(j)]
            head = step * PER_STEP + j
            log_total = lse[pl.ds(head, 1), :]
            row_dots = rows[pl.ds(head, 1), :]
            p = jnp.exp2(dot_last(k[...], queries) * SCALE2 + key_bias(frames, at, limits, -log_total))
            value_dots = dot_last(v[...], grads)
            dk_part = dk_part + dot((p * (value_dots - row_dots)).astype(jnp.bfloat16), queries)
            dv_part = dv_part + dot(p.astype(jnp.bfloat16), grads)

        @pl.when(first)
        def _():
            dk[...] = dk_part
            dv[...] = dv_part

        @pl.when(jnp.logical_not(first))
        def _():
            dk[...] += dk_part
            dv[...] += dv_part


def attention_call(kernel, name, products, frames, limit, stats, both, keys, out_specs, out_shape, scratch):
    queries, key_rows = both.shape[0], keys[0].shape[0]
    steps = both.shape[1] // (2 * HEAD_DIM * PER_STEP)
    work = steps * PER_STEP * queries * 2 * key_rows
    whole = [pl.BlockSpec(x.shape, lambda i, n=x.ndim: (0,) * n) for x in (limit,) + stats]
    q = pl.BlockSpec((queries, PER_STEP * HEAD_DIM), lambda i: (0, i))
    do = pl.BlockSpec((queries, PER_STEP * HEAD_DIM), lambda i: (0, steps + i))
    kv = pl.BlockSpec((key_rows, HEAD_DIM), lambda i: (0, i // (GROUP // PER_STEP)))
    return pl.pallas_call(
        kernel,
        grid=(steps,),
        in_specs=[pl.BlockSpec(memory_space=pltpu.SMEM)] + whole + [q, do, kv, kv, kv, kv],
        out_specs=out_specs(q, kv),
        out_shape=out_shape,
        scratch_shapes=scratch,
        cost_estimate=pl.CostEstimate(
            flops=2 * products * work * HEAD_DIM, bytes_accessed=4 * both.size, transcendentals=work
        ),
        name=name,
    )(frames, limit, *stats, both, both, *keys)


def forward_stats(frames, limit, both, keys):
    queries, key_rows = both.shape[0], keys[0].shape[0]
    shape = (2, both.shape[1] // (2 * HEAD_DIM), queries)
    return attention_call(
        forward_kernel, "forward_stats", 2, frames, limit, (), both, keys,
        lambda q, kv: pl.BlockSpec(shape, lambda i: (0, 0, 0)),
        jax.ShapeDtypeStruct(shape, jnp.float32),
        [pltpu.VMEM((PER_STEP, 2, key_rows, queries), jnp.float32)],
    )


def query_sums(frames, limit, stats, both, keys):
    queries, key_rows = both.shape[0], keys[0].shape[0]
    heads = stats.shape[2]
    return attention_call(
        query_kernel, "query_sums", 3, frames, limit, (stats,), both, keys,
        lambda q, kv: q,
        jax.ShapeDtypeStruct((queries, heads * HEAD_DIM), jnp.float32),
        [
            pltpu.VMEM((queries, 2 * key_rows), jnp.float32),
            pltpu.VMEM((heads // PER_STEP, queries, HEAD_DIM), jnp.float32),
        ],
    )


def key_value_sums(frames, limit, stats, both, keys):
    row = pltpu.VMEM(stats.shape[2:], jnp.float32)
    return attention_call(
        keys_kernel, "key_value_sums", 4, frames, limit, (stats,), both, keys,
        lambda q, kv: [kv] * 4,
        [jax.ShapeDtypeStruct(keys[0].shape, jnp.float32)] * 4,
        [row, row],
    )


def gather_copies(x, axes):
    count = lax.axis_size(axes)
    copies = jnp.broadcast_to(x[None], (count,) + x.shape)
    return lax.all_to_all(copies, axes, 0, 0, tiled=True)


def swap_z(x):
    return lax.ppermute(x, "vz", [(0, 1), (1, 0)])


def line_shift(x, shift):
    count = lax.axis_size("vy")
    return lax.ppermute(x, "vy", [(i, (i + shift) % count) for i in range(count)])


def text_kernel(line, rows, own, below0, below1, above0, above1, far0, far1, out):
    count = out.shape[0]
    half = far0.shape[0]
    me = line[0]
    first, second = rows[:, :half], rows[:, half:]
    out[me] = dot(first, own[:half]) + dot(second, own[half:])
    out[lax.rem(me + count - 1, count)] = dot(first, below0[...]) + dot(second, below1[...])
    out[lax.rem(me + 1, count)] = dot(first, above0[...]) + dot(second, above1[...])
    out[lax.rem(me + 2, count)] = dot(first, far0[...]) + dot(second, far1[...])


def text_product(rows, weights):
    count = lax.axis_size("vy")
    depth, columns = weights[0].shape
    vmem = pl.BlockSpec(memory_space=pltpu.VMEM)
    return pl.pallas_call(
        text_kernel,
        in_specs=[pl.BlockSpec(memory_space=pltpu.SMEM)] + [vmem] * 8,
        out_specs=vmem,
        out_shape=jax.ShapeDtypeStruct((count, rows.shape[0], columns), jnp.float32),
        cost_estimate=pl.CostEstimate(
            flops=2 * rows.size * count * columns, bytes_accessed=2 * count * depth * columns, transcendentals=0
        ),
        name="text_product",
    )(lax.axis_index("vy").reshape(1), rows, *weights)


def shards(text_queries, visual_keys, visual_values, out_grad, query_frame, block_frame, q_weight):
    z = lax.axis_index("vz")
    plane = lax.axis_index(PLANE)
    side = lax.axis_size(PLANE)
    query_rows = text_queries.shape[0]
    blocks = visual_keys.shape[0] // BLOCK
    other_keys, other_values = swap_z(visual_keys), swap_z(visual_values)
    own_frames = lax.dynamic_slice_in_dim(block_frame, (z * side + plane) * blocks, blocks)
    other_frames = lax.dynamic_slice_in_dim(block_frame, ((1 - z) * side + plane) * blocks, blocks)
    frames = jnp.concatenate([own_frames, other_frames])
    queries = query_rows * side
    limit = lax.dynamic_slice_in_dim(query_frame, z * queries, queries)[None]
    own_both = jnp.concatenate([text_queries, out_grad], axis=1)
    both = gather_copies(own_both, PLANE).reshape(queries, own_both.shape[1])
    both, other_keys, other_values, q_weight = lax.optimization_barrier(
        (both, other_keys, other_values, q_weight)
    )
    keys = (visual_keys, visual_values, other_keys, other_values)
    depth = q_weight.shape[0] // 2
    below0, above0 = line_shift(q_weight[:depth], 1), line_shift(q_weight[:depth], -1)
    stats, below0, above0 = lax.optimization_barrier(
        (forward_stats(frames, limit, both, keys), below0, above0)
    )
    stats, later = lax.optimization_barrier((gather_copies(stats, PLANE), q_weight[depth:]))
    below1, above1 = line_shift(later, 1), line_shift(later, -1)
    dq, below0, below1, above1 = lax.optimization_barrier(
        (query_sums(frames, limit, stats, both, keys), below0, below1, above1)
    )
    terms = lax.all_to_all(dq.reshape(side, query_rows, -1), PLANE, 0, 0, tiled=True)
    dk0, dv0, dk1, dv1 = key_value_sums(frames, limit, stats, both, keys)
    query_grad = jnp.sum(terms, axis=0).astype(jnp.bfloat16)
    rows = gather_copies(query_grad, ("vz", "vx"))
    key_grad = ((dk0 + swap_z(dk1)) * SCALE).astype(jnp.bfloat16)
    value_grad = (dv0 + swap_z(dv1)).astype(jnp.bfloat16)
    far0, far1 = line_shift(below0, 1), line_shift(above1, -1)
    weights = (q_weight, below0, below1, above0, above1, far0, far1)
    text = text_product(rows.reshape(-1, rows.shape[-1]), weights)
    lines, parts = lax.axis_size("vy"), lax.axis_size("head")
    text = text.reshape(lines * parts, text.shape[1] // parts, text.shape[2])
    text = lax.all_to_all(text, ("vy", "head"), 0, 0, tiled=True)
    text = jnp.sum(text.reshape(lines, parts, -1, query_rows, text.shape[2]), axis=1)
    text_grad = text.transpose(1, 0, 2, 3).reshape(-1, text.shape[3]).astype(jnp.bfloat16)
    return (query_grad, key_grad, value_grad, text_grad)


def solution(mesh):
    split = Mesh(
        mesh.devices.reshape(2, 4, 4, mesh.shape["head"]), ("vz", "vx", "vy", "head")
    )
    placed = (
        P(VIDEO, "head"),
        P(VIDEO, "head"),
        P(VIDEO, "head"),
        P(VIDEO, "head"),
        P(),
        P(),
        P("head", VIDEO),
    )
    return jax.shard_map(
        shards,
        mesh=split,
        in_specs=placed,
        out_specs=(P(VIDEO, "head"), P(VIDEO, "head"), P(VIDEO, "head"), P("head", VIDEO)),
        check_vma=False,
    )
```

time: 179 us -> 153 us (0.85)
  blocking collectives: 29.8 us -> 12.9 us
  starting transfers between devices: 33 us -> 48 us
  between operations: 14.1 us -> 0.77 us
  waiting for transfers between devices: 54.5 us -> 41.6 us
  local copies, waits for them, and re-layouts: 4.01 us -> 8.1 us
  Pallas kernels: 39.6 us -> 37.8 us
    ppermute x4, waiting for transfers between devices: 32.9 us -> 10.6 us  [swap_z(): return lax.ppermute(x, 'vz', [(0, 1), (1, 0)])]
    all_to_all x2 -> x1, blocking collectives: 29.8 us -> 12.9 us  [gather_copies(): return lax.all_to_all(copies, axes, 0, 0, tiled=True)]
    all_to_all x1 -> x2, starting transfers between devices: 7.73 us -> 15 us  [gather_copies(): return lax.all_to_all(copies, axes, 0, 0, tiled=True)]
    ppermute x0 -> x6, starting transfers between devices: none -> 5.68 us  [line_shift(): lax.ppermute(x, 'vy', [(i, (i + shift) % count) for i in range(count)])]
    all_to_all x1 -> x2, waiting for transfers between devices: 12.8 us -> 18 us  [gather_copies(): return lax.all_to_all(copies, axes, 0, 0, tiled=True)]
    all_to_all x1, starting transfers between devices: 8.61 us -> 3.88 us  [shards(): lax.all_to_all(dq.reshape(side, query_rows, -1), PLANE, 0, 0, tiled=True)]
    all_to_all x1, starting transfers between devices: 9.08 us -> 13 us  [shards(): text = lax.all_to_all(text, ('vy', 'head'), 0, 0, tiled=True)]
    all_to_all x1, waiting for transfers between devices: 0.08 us -> 3.54 us  [shards(): lax.all_to_all(dq.reshape(side, query_rows, -1), PLANE, 0, 0, tiled=True)]
  transfers between devices with their start and end apart: 8 -> 14, of which waited for: 7 -> 8; matrix products, arithmetic and copies ran while one was open for 2% -> 3% of each run, Pallas kernels for 20% -> 25%
where the time goes in v4:
time: 153 us; the launch traced here: 152 us
  starting transfers between devices  48 us (31%)
  waiting for transfers between devices  41.6 us (27%)
  Pallas kernels  37.8 us (25%)
  blocking collectives  12.9 us (8%)
  local copies, waits for them, and re-layouts  8.1 us (5%)
  other arithmetic  3.21 us (2%)
    pallas_call x3, Pallas kernels, attention_call(): pl.pallas_call(kernel, grid=(steps,), in_specs=[pl.BlockSpec(memory_space...  33.9 us
    all_to_all x2, waiting for transfers between devices, gather_copies(): return lax.all_to_all(copies, axes, 0, 0, tiled=True)  18 us
    all_to_all x2, starting transfers between devices, gather_copies(): return lax.all_to_all(copies, axes, 0, 0, tiled=True)  15 us
    all_to_all x1, starting transfers between devices, shards(): text = lax.all_to_all(text, ('vy', 'head'), 0, 0, tiled=True)  13 us
    all_to_all x1, blocking collectives, gather_copies(): return lax.all_to_all(copies, axes, 0, 0, tiled=True)  12.9 us
    ppermute x4, waiting for transfers between devices, swap_z(): return lax.ppermute(x, 'vz', [(0, 1), (1, 0)])  10.6 us
    ppermute x4, starting transfers between devices, swap_z(): return lax.ppermute(x, 'vz', [(0, 1), (1, 0)])  10.4 us
    all_to_all x1, waiting for transfers between devices, shards(): text = lax.all_to_all(text, ('vy', 'head'), 0, 0, tiled=True)  8.08 us
  transfers between devices with their start and end apart: 14, of which 8 were waited for; matrix products, arithmetic and copies ran while one was open for 3% of the time, Pallas kernels for 25%

profile of v4, /device:TPU:1, one launch (start us, length us, event | category | flops | bytes accessed | tf_op | source)
XLA Modules:
  0.0 152.4 jit_solution(6229498453352197960)
XLA Ops:
  0.6 0.9 pad_maximum_fusion
  1.5 1.6 %broadcast_in_dim.9 = bf16[16,16,4096]{2,1,0:T(8,128)(2,1)} broadcast(bf16[16,4096]{1,0:T(8,128)(2,1)S(1)} %pad_maximum_fusion), dimensions={1,2} | broadcast | bytes 2228224 | tf_op jit(solution)/shard_map/broadcast_in_dim | solution.py:208
  3.1 7.7 %all-to-all-start = ((bf16[16,16,4096]{2,1,0:T(8,128)(2,1)}), bf16[16,16,4096]{2,1,0:T(8,128)(2,1)S(1)}, u32[]{:S(2)}, u32[]{:S(2)}) async-start(bf16[16,16,4096]{2,1,0:T(8,128)(2,1)} %broadcast_in_dim.9), calls=%async_computation | async-start | bytes 4194304 | tf_op jit(solution)/shard_map/all_to_all | solution.py:209
  10.8 0.0 copy-done.12
  10.8 0.0 copy-start.11
  10.8 0.0 copy-start.10
  10.9 3.7 %collective-permute-start = (bf16[512,256]{1,0:T(8,128)(2,1)S(1)}, bf16[512,256]{1,0:T(8,128)(2,1)S(1)}, u32[]{:S(2)}, u32[]{:S(2)}) collective-permute-start(bf16[512,256]{1,0:T(8,128)(2,1)S(1)} %copy-done.12), channel_id=1, source_target_pairs={{0,64},{64,0},{1,65},{65,1},{2,66},{66,2},{3,67},{67,3},{4,68},{68... | collective-permute-start | bytes 786440 | tf_op jit(solution)/shard_map/ppermute | solution.py:213
  14.5 0.1 collective-permute-start.1
  14.6 5.6 %collective-permute-done.k1 = bf16[512,256]{1,0:T(8,128)(2,1)S(1)} collective-permute-done((bf16[512,256]{1,0:T(8,128)(2,1)S(1)}, bf16[512,256]{1,0:T(8,128)(2,1)S(1)}, u32[]{:S(2)}, u32[]{:S(2)}) %collective-permute-start) | collective-permute-done | bytes 262176 | tf_op jit(solution)/shard_map/ppermute | solution.py:213
  20.2 0.7 copy-done.13
  20.9 5.0 %collective-permute-done.1.v1 = bf16[512,256]{1,0:T(8,128)(2,1)} collective-permute-done((bf16[512,256]{1,0:T(8,128)(2,1)}, bf16[512,256]{1,0:T(8,128)(2,1)}, u32[]{:S(2)}, u32[]{:S(2)}) %collective-permute-start.1) | collective-permute-done | bytes 262176 | tf_op jit(solution)/shard_map/ppermute | solution.py:213
  26.0 12.7 %all-to-all-done = bf16[16,16,4096]{2,1,0:T(8,128)(2,1)S(1)} async-done(((bf16[16,16,4096]{2,1,0:T(8,128)(2,1)}), bf16[16,16,4096]{2,1,0:T(8,128)(2,1)S(1)}, u32[]{:S(2)}, u32[]{:S(2)}) %all-to-all-start) | async-done | bytes 2097184 | tf_op jit(solution)/shard_map/all_to_all | solution.py:209
  38.7 0.0 copy-done
  38.7 1.1 fusion
  39.8 0.4 collective-permute-start.3
  40.2 1.1 collective-permute-start.2
  41.3 0.0 copy-done.11
  41.3 0.6 dynamic_slice.11
  41.9 0.0 copy-done.10
  41.9 0.1 fusion.1
  42.0 0.7 pad_add_fusion.frames
  42.7 0.0 copy-done.1
  42.7 8.9 %forward_stats.1 = f32[2,16,256]{2,1,0:T(8,128)} custom-call(s32[8]{0:T(128)} %pad_add_fusion.frames, s32[1,256]{1,0:T(1,128)} %bitcast.23, bf16[256,4096]{1,0:T(8,128)(2,1)} %bitcast.11, bf16[256,4096]{1,0:T(8,128)(2,1)} %bitcast.12, bf16[512,256]{1,0:T(8,128)(2,1)} %k0.5, bf16[512,256]{1,0:T(8,128)(2,1)} %v0.5, bf16[512,256]{1,0:T(8,128)(2,1)} %copy-done.13, ...), custom_call_target="tpu_custom_call" | custom-call | flops 2147483648 | bytes 4194304 | tf_op jit(solution)/shard_map/forward_stats/pallas_call | solution.py:157
  51.6 0.0 collective-permute-done.3.above0
  51.6 0.0 copy-start.6
  51.6 0.5 collective-permute-done.2.below0
  52.1 0.8 broadcast_in_dim.10
  52.9 12.9 %all_to_all.25.stats = f32[16,2,16,256]{3,2,1,0:T(8,128)} all-to-all(f32[16,2,16,256]{3,2,1,0:T(8,128)S(1)} %broadcast_in_dim.10), channel_id=1, replica_groups=mesh['vz'=2,'vx'=4,'vy'=4,'head'=4] {'vx','vy'}, dimensions={0} | all-to-all | bytes 1048576 | tf_op jit(solution)/shard_map/all_to_all | solution.py:209
  65.9 0.0 copy-done.5
  65.9 0.3 collective-permute-start.5
  66.2 1.2 collective-permute-start.4
  67.3 11.7 %query_sums.1 = f32[256,2048]{1,0:T(8,128)} custom-call(s32[8]{0:T(128)} %pad_add_fusion.frames, s32[1,256]{1,0:T(1,128)} %bitcast.24, f32[16,2,16,256]{3,2,1,0:T(8,128)} %all_to_all.25.stats, bf16[256,4096]{1,0:T(8,128)(2,1)} %bitcast.13, bf16[256,4096]{1,0:T(8,128)(2,1)} %bitcast.14, bf16[512,256]{1,0:T(8,128)(2,1)} %k0.5, bf16[512,256]{1,0:T(8,128)(2,1)} %v0.5, ...), custom_call_target="tpu_custom_call" | custom-call | flops 3221225472 | bytes 4194304 | tf_op jit(solution)/shard_map/query_sums/pallas_call | solution.py:157
  79.1 0.0 copy-done.6
  79.1 0.0 collective-permute-done.5.above1
  79.1 0.0 collective-permute-done.4.below1
  79.1 0.0 copy-start.7
  79.1 0.8 copy-done.7
  80.0 3.9 %all-to-all-start.2 = ((f32[16,16,2048]{2,1,0:T(8,128)}), f32[16,16,2048]{2,1,0:T(8,128)S(1)}, u32[]{:S(2)}, u32[]{:S(2)}) async-start(f32[16,16,2048]{2,1,0:T(8,128)} %bitcast.17), calls=%async_computation.2 | async-start | bytes 4194304 | tf_op jit(solution)/shard_map/all_to_all | solution.py:276
  83.8 1.4 collective-permute-start.8
  85.2 1.4 collective-permute-start.9
  86.6 13.2 %key_value_sums.1 = (f32[512,256]{1,0:T(8,128)}, f32[512,256]{1,0:T(8,128)}, f32[512,256]{1,0:T(8,128)}, f32[512,256]{1,0:T(8,128)}) custom-call(s32[8]{0:T(128)} %pad_add_fusion.frames, s32[1,256]{1,0:T(1,128)} %bitcast.25, f32[16,2,16,256]{3,2,1,0:T(8,128)} %all_to_all.25.stats, bf16[256,4096]{1,0:T(8,128)(2,1)} %bitcast.15, bf16[256,4096]{1,0:T(8,128)(2,1)} %bitcast.16, ...), custom_call_target="tpu_custom_call" | custom-call | flops 4294967296 | bytes 4194304 | tf_op jit(solution)/shard_map/key_value_sums/pallas_call | solution.py:157
  99.8 3.7 %collective-permute-start.6 = (f32[512,256]{1,0:T(8,128)}, f32[512,256]{1,0:T(8,128)S(1)}, u32[]{:S(2)}, u32[]{:S(2)}) collective-permute-start(f32[512,256]{1,0:T(8,128)} %get-tuple-element.31), channel_id=1, source_target_pairs={{0,64},{64,0},{1,65},{65,1},{2,66},{66,2},{3,67},{67,3},{4,68},{68... | collective-permute-start | bytes 1572872 | tf_op jit(solution)/shard_map/ppermute | solution.py:213
  103.5 3.5 %all-to-all-done.2 = f32[16,16,2048]{2,1,0:T(8,128)S(1)} async-done(((f32[16,16,2048]{2,1,0:T(8,128)}), f32[16,16,2048]{2,1,0:T(8,128)S(1)}, u32[]{:S(2)}, u32[]{:S(2)}) %all-to-all-start.2) | async-done | bytes 2097184 | tf_op jit(solution)/shard_map/all_to_all | solution.py:276
  107.0 0.1 reduce_sum.18
  107.1 0.0 copy-start.9
  107.2 0.9 broadcast_in_dim.11
  108.0 7.3 %all-to-all-start.3 = ((bf16[8,16,2048]{2,1,0:T(8,128)(2,1)}), bf16[8,16,2048]{2,1,0:T(8,128)(2,1)S(1)}, u32[]{:S(2)}, u32[]{:S(2)}) async-start(bf16[8,16,2048]{2,1,0:T(8,128)(2,1)} %broadcast_in_dim.11), calls=%async_computation.3 | async-start | bytes 1048576 | tf_op jit(solution)/shard_map/all_to_all | solution.py:209
  115.3 3.0 %collective-permute-start.7 = (f32[512,256]{1,0:T(8,128)}, f32[512,256]{1,0:T(8,128)S(1)}, u32[]{:S(2)}, u32[]{:S(2)}) collective-permute-start(f32[512,256]{1,0:T(8,128)} %get-tuple-element.33), channel_id=1, source_target_pairs={{0,64},{64,0},{1,65},{65,1},{2,66},{66,2},{3,67},{67,3},{4,68},{68... | collective-permute-start | bytes 1572872 | tf_op jit(solution)/shard_map/ppermute | solution.py:213
  118.3 0.8 collective-permute-done.8.far0
  119.1 0.0 collective-permute-done.9.far1
  119.1 5.3 %all-to-all-done.3 = bf16[8,16,2048]{2,1,0:T(8,128)(2,1)S(1)} async-done(((bf16[8,16,2048]{2,1,0:T(8,128)(2,1)}), bf16[8,16,2048]{2,1,0:T(8,128)(2,1)S(1)}, u32[]{:S(2)}, u32[]{:S(2)}) %all-to-all-start.3) | async-done | bytes 524320 | tf_op jit(solution)/shard_map/all_to_all | solution.py:209
  124.4 0.0 copy-done.8
  124.4 0.8 copy-done.2
  125.2 3.9 %text_product.1 = f32[4,128,256]{2,1,0:T(8,128)} custom-call(s32[1]{0:T(128)} %bitcast.3.line, bf16[128,2048]{1,0:T(8,128)(2,1)} %bitcast.20, bf16[2048,256]{1,0:T(8,128)(2,1)} %own, bf16[1024,256]{1,0:T(8,128)(2,1)} %collective-permute-done.2.below0, bf16[1024,256]{1,0:T(8,128)(2,1)} %copy-done.7, bf16[1024,256]{1,0:T(8,128)(2,1)} %copy-done.6, ...), custom_call_target="tpu_custom_call" | custom-call | flops 536870912 | bytes 4194304 | tf_op jit(solution)/shard_map/text_product/pallas_call | solution.py:236
  129.1 0.0 copy-done.9
  129.1 13.0 %all-to-all-start.4 = ((f32[16,32,256]{2,1,0:T(8,128)}), f32[16,32,256]{2,1,0:T(8,128)S(1)}, u32[]{:S(2)}, u32[]{:S(2)}) async-start(f32[16,32,256]{2,1,0:T(8,128)} %bitcast.19), calls=%async_computation.4 | async-start | bytes 1048576 | tf_op jit(solution)/shard_map/all_to_all | solution.py:287
  142.0 0.0 collective-permute-done.6
  142.1 0.0 copy-done.4
  142.1 0.8 multiply_convert_fusion
  142.8 0.0 collective-permute-done.7
  142.8 0.0 copy-done.3
  142.8 0.8 add_convert_fusion
  143.6 8.1 %all-to-all-done.4 = f32[16,32,256]{2,1,0:T(8,128)S(1)} async-done(((f32[16,32,256]{2,1,0:T(8,128)}), f32[16,32,256]{2,1,0:T(8,128)S(1)}, u32[]{:S(2)}, u32[]{:S(2)}) %all-to-all-start.4) | async-done | bytes 524320 | tf_op jit(solution)/shard_map/all_to_all | solution.py:287
  151.7 0.6 copy.11
  (10 shorter events, 0.1 us)
Async XLA Ops:
  3.1 7.7 %copy-start.12 = (bf16[512,256]{1,0:T(8,128)(2,1)S(1)}, bf16[512,256]{1,0:T(8,128)(2,1)}, u32[]{:S(2)}) copy-start(bf16[512,256]{1,0:T(8,128)(2,1)} %k0.5) | copy-start | bytes 786436
  3.1 35.6 %copy-start = (bf16[2048,256]{1,0:T(8,128)(2,1)S(1)}, bf16[2048,256]{1,0:T(8,128)(2,1)}, u32[]{:S(2)}) copy-start(bf16[2048,256]{1,0:T(8,128)(2,1)} %own) | copy-start | bytes 3145732
  3.1 35.6 %all-to-all-start = ((bf16[16,16,4096]{2,1,0:T(8,128)(2,1)}), bf16[16,16,4096]{2,1,0:T(8,128)(2,1)S(1)}, u32[]{:S(2)}, u32[]{:S(2)}) async-start(bf16[16,16,4096]{2,1,0:T(8,128)(2,1)} %broadcast_in_dim.9), calls=%async_computation | async-start | bytes 4194304 | tf_op jit(solution)/shard_map/all_to_all | solution.py:209
  10.8 30.5 %copy-start.11 = (s32[512]{0:T(512)S(1)}, s32[512]{0:T(512)}, u32[]{:S(2)}) copy-start(s32[512]{0:T(512)} %param.11) | copy-start | bytes 6148
  10.8 31.1 %copy-start.10 = (s32[128]{0:T(128)S(1)}, s32[128]{0:T(128)}, u32[]{:S(2)}) copy-start(s32[128]{0:T(128)} %param.12) | copy-start | bytes 1540
  10.9 9.4 %collective-permute-start = (bf16[512,256]{1,0:T(8,128)(2,1)S(1)}, bf16[512,256]{1,0:T(8,128)(2,1)S(1)}, u32[]{:S(2)}, u32[]{:S(2)}) collective-permute-start(bf16[512,256]{1,0:T(8,128)(2,1)S(1)} %copy-done.12), channel_id=1, source_target_pairs={{0,64},{64,0},{1,65},{65,1},{2,66},{66,2},{3,67},{67,3},{4,68},{68... | collective-permute-start | bytes 786440 | tf_op jit(solution)/shard_map/ppermute | solution.py:213
  14.5 11.4 %collective-permute-start.1 = (bf16[512,256]{1,0:T(8,128)(2,1)}, bf16[512,256]{1,0:T(8,128)(2,1)}, u32[]{:S(2)}, u32[]{:S(2)}) collective-permute-start(bf16[512,256]{1,0:T(8,128)(2,1)} %v0.5), channel_id=1, source_target_pairs={{0,64},{64,0},{1,65},{65,1},{2,66},{66,2},{3,67},{67,3},{4,68},{68... | collective-permute-start | bytes 786440 | tf_op jit(solution)/shard_map/ppermute | solution.py:213
  20.2 0.7 copy-start.13
  38.7 4.0 %copy-start.1 = (bf16[16,16,4096]{2,1,0:T(8,128)(2,1)}, bf16[16,16,4096]{2,1,0:T(8,128)(2,1)S(1)}, u32[]{:S(2)}) copy-start(bf16[16,16,4096]{2,1,0:T(8,128)(2,1)S(1)} %all-to-all-done) | copy-start | bytes 6291460
  39.8 11.8 %collective-permute-start.3 = (bf16[1024,256]{1,0:T(8,128)(2,1)}, bf16[1024,256]{1,0:T(8,128)(2,1)S(1)}, u32[]{:S(2)}, u32[]{:S(2)}) collective-permute-start(bf16[1024,256]{1,0:T(8,128)(2,1)} %get-tuple-element.39), channel_id=1, source_target_pairs={{0,12},{4,0},{8,4},{12,8},{1,13},{5,1},{9,5},{13,9},{2,14},{6,2},{... | collective-permute-start | bytes 1572872 | tf_op jit(solution)/shard_map/ppermute | solution.py:218
  40.2 11.9 %collective-permute-start.2 = (bf16[1024,256]{1,0:T(8,128)(2,1)}, bf16[1024,256]{1,0:T(8,128)(2,1)}, u32[]{:S(2)}, u32[]{:S(2)}) collective-permute-start(bf16[1024,256]{1,0:T(8,128)(2,1)} %get-tuple-element.39), channel_id=1, source_target_pairs={{0,4},{4,8},{8,12},{12,0},{1,5},{5,9},{9,13},{13,1},{2,6},{6,10},{... | collective-permute-start | bytes 1572872 | tf_op jit(solution)/shard_map/ppermute | solution.py:218
  42.7 23.2 %copy-start.5 = (bf16[1024,256]{1,0:T(8,128)(2,1)S(1)}, bf16[1024,256]{1,0:T(8,128)(2,1)}, u32[]{:S(2)}) copy-start(bf16[1024,256]{1,0:T(8,128)(2,1)} %get-tuple-element.28) | copy-start | bytes 1572868
  51.6 27.5 %copy-start.6 = (bf16[1024,256]{1,0:T(8,128)(2,1)}, bf16[1024,256]{1,0:T(8,128)(2,1)S(1)}, u32[]{:S(2)}) copy-start(bf16[1024,256]{1,0:T(8,128)(2,1)S(1)} %collective-permute-done.3.above0) | copy-start | bytes 1572868
  65.9 13.2 %collective-permute-start.5 = (bf16[1024,256]{1,0:T(8,128)(2,1)S(1)}, bf16[1024,256]{1,0:T(8,128)(2,1)}, u32[]{:S(2)}, u32[]{:S(2)}) collective-permute-start(bf16[1024,256]{1,0:T(8,128)(2,1)S(1)} %copy-done.5), channel_id=1, source_target_pairs={{0,12},{4,0},{8,4},{12,8},{1,13},{5,1},{9,5},{13,9},{2,14},{6,2},{... | collective-permute-start | bytes 1572872 | tf_op jit(solution)/shard_map/ppermute | solution.py:218
  66.2 12.9 %collective-permute-start.4 = (bf16[1024,256]{1,0:T(8,128)(2,1)S(1)}, bf16[1024,256]{1,0:T(8,128)(2,1)S(1)}, u32[]{:S(2)}, u32[]{:S(2)}) collective-permute-start(bf16[1024,256]{1,0:T(8,128)(2,1)S(1)} %copy-done.5), channel_id=1, source_target_pairs={{0,4},{4,8},{8,12},{12,0},{1,5},{5,9},{9,13},{13,1},{2,6},{6,10},{... | collective-permute-start | bytes 1572872 | tf_op jit(solution)/shard_map/ppermute | solution.py:218
  79.1 0.9 copy-start.7
  80.0 27.1 %all-to-all-start.2 = ((f32[16,16,2048]{2,1,0:T(8,128)}), f32[16,16,2048]{2,1,0:T(8,128)S(1)}, u32[]{:S(2)}, u32[]{:S(2)}) async-start(f32[16,16,2048]{2,1,0:T(8,128)} %bitcast.17), calls=%async_computation.2 | async-start | bytes 4194304 | tf_op jit(solution)/shard_map/all_to_all | solution.py:276
  83.8 35.3 %collective-permute-start.8 = (bf16[1024,256]{1,0:T(8,128)(2,1)}, bf16[1024,256]{1,0:T(8,128)(2,1)S(1)}, u32[]{:S(2)}, u32[]{:S(2)}) collective-permute-start(bf16[1024,256]{1,0:T(8,128)(2,1)} %collective-permute-done.2.below0), channel_id=1, source_target_pairs={{0,4},{4,8},{8,12},{12,0},{1,5},{5,9},{9,13},{13,1},{2,6},{6,10},{... | collective-permute-start | bytes 1572872 | tf_op jit(solution)/shard_map/ppermute | solution.py:218
  85.2 33.9 %collective-permute-start.9 = (bf16[1024,256]{1,0:T(8,128)(2,1)}, bf16[1024,256]{1,0:T(8,128)(2,1)}, u32[]{:S(2)}, u32[]{:S(2)}) collective-permute-start(bf16[1024,256]{1,0:T(8,128)(2,1)} %collective-permute-done.5.above1), channel_id=1, source_target_pairs={{0,12},{4,0},{8,4},{12,8},{1,13},{5,1},{9,5},{13,9},{2,14},{6,2},{... | collective-permute-start | bytes 1572872 | tf_op jit(solution)/shard_map/ppermute | solution.py:218
  99.8 42.2 %collective-permute-start.6 = (f32[512,256]{1,0:T(8,128)}, f32[512,256]{1,0:T(8,128)S(1)}, u32[]{:S(2)}, u32[]{:S(2)}) collective-permute-start(f32[512,256]{1,0:T(8,128)} %get-tuple-element.31), channel_id=1, source_target_pairs={{0,64},{64,0},{1,65},{65,1},{2,66},{66,2},{3,67},{67,3},{4,68},{68... | collective-permute-start | bytes 1572872 | tf_op jit(solution)/shard_map/ppermute | solution.py:213
  107.1 21.9 %copy-start.9 = (bf16[16,2048]{1,0:T(8,128)(2,1)}, bf16[16,2048]{1,0:T(8,128)(2,1)S(1)}, u32[]{:S(2)}) copy-start(bf16[16,2048]{1,0:T(8,128)(2,1)S(1)} %reduce_sum.18) | copy-start | bytes 196612
  108.0 16.4 %all-to-all-start.3 = ((bf16[8,16,2048]{2,1,0:T(8,128)(2,1)}), bf16[8,16,2048]{2,1,0:T(8,128)(2,1)S(1)}, u32[]{:S(2)}, u32[]{:S(2)}) async-start(bf16[8,16,2048]{2,1,0:T(8,128)(2,1)} %broadcast_in_dim.11), calls=%async_computation.3 | async-start | bytes 1048576 | tf_op jit(solution)/shard_map/all_to_all | solution.py:209
  115.3 27.5 %collective-permute-start.7 = (f32[512,256]{1,0:T(8,128)}, f32[512,256]{1,0:T(8,128)S(1)}, u32[]{:S(2)}, u32[]{:S(2)}) collective-permute-start(f32[512,256]{1,0:T(8,128)} %get-tuple-element.33), channel_id=1, source_target_pairs={{0,64},{64,0},{1,65},{65,1},{2,66},{66,2},{3,67},{67,3},{4,68},{68... | collective-permute-start | bytes 1572872 | tf_op jit(solution)/shard_map/ppermute | solution.py:213
  119.1 5.3 %copy-start.8 = (bf16[1024,256]{1,0:T(8,128)(2,1)}, bf16[1024,256]{1,0:T(8,128)(2,1)S(1)}, u32[]{:S(2)}) copy-start(bf16[1024,256]{1,0:T(8,128)(2,1)S(1)} %collective-permute-done.8.far0) | copy-start | bytes 1572868
  124.4 0.8 copy-start.2
  125.2 16.9 %copy-start.4 = (f32[512,256]{1,0:T(8,128)S(1)}, f32[512,256]{1,0:T(8,128)}, u32[]{:S(2)}) copy-start(f32[512,256]{1,0:T(8,128)} %get-tuple-element.30) | copy-start | bytes 1572868
  129.1 13.8 %copy-start.3 = (f32[512,256]{1,0:T(8,128)S(1)}, f32[512,256]{1,0:T(8,128)}, u32[]{:S(2)}) copy-start(f32[512,256]{1,0:T(8,128)} %get-tuple-element.32) | copy-start | bytes 1572868
  129.1 22.6 %all-to-all-start.4 = ((f32[16,32,256]{2,1,0:T(8,128)}), f32[16,32,256]{2,1,0:T(8,128)S(1)}, u32[]{:S(2)}, u32[]{:S(2)}) async-start(f32[16,32,256]{2,1,0:T(8,128)} %bitcast.19), calls=%async_computation.4 | async-start | bytes 1048576 | tf_op jit(solution)/shard_map/all_to_all | solution.py:287
